TPU v7x, 512 devices: a whole 4x4x16 slice. The times are simulated.
512 devices in a mesh: tok: 64 (over z, y), head: 8 (over x, core).
Axes of the slice: x: 4, y: 4, z: 16, core: 2. Of those that a mesh axis runs over, the one named last changes fastest.
Arguments:
- inputs: bfloat16 [2, 16384, 2048], P(None, 'tok', 'head'), may hold values from -6 to 6
- probe_projector: bfloat16 [2048, 2048], P(None, 'head'), may hold values from -0.125 to 0.125
- address_projector: bfloat16 [2048, 2048], P(None, 'head'), may hold values from -0.125 to 0.125
- payload_projector: bfloat16 [2048, 2048], P(None, 'head'), may hold values from -0.125 to 0.125
- checkpoints: bfloat16 [2, 3, 8, 256, 512], P(None, None, 'head', 'tok'), may hold values from -0.375 to 0.375
- out_grad: bfloat16 [2, 16384, 2048], P(None, 'tok', 'head'), may hold values from -16 to 16
- adjoint: float32 [3, 8, 256, 512], P(None, 'head', 'tok'), may hold values from -96 to 96
- inner_rate: float32 [8], P('head'), may hold values from 0.25 to 4
Outputs:
- input_grad: bfloat16 [2, 16384, 2048], P(None, 'tok', 'head')
All inputs are finite; a program needn't handle non-finite values.
Results may differ from a plain program's by a relative error of at most 0.014.
Values may be sent and summed in bfloat16 or wider, within the bound.
A program may use at most 64 MiB of HBM per device.

v0:
```python
import jax
import jax.numpy as jnp
from jax import lax
from jax.sharding import Mesh
from jax.sharding import PartitionSpec as P

TOK = ("tok_0", "tok_1")


def laid_out(pieces, dim):
    shape = list(pieces.shape[1:])
    shape[dim] *= pieces.shape[0]
    return jnp.moveaxis(pieces, 0, dim).reshape(shape)


def copy_for_each(value, axis):
    copies = jnp.broadcast_to(value, (lax.axis_size(axis), *value.shape))
    return lax.all_to_all(copies, axis, split_axis=0, concat_axis=0, tiled=True)


def gathered_copies(value, axis, dim):
    return laid_out(copy_for_each(value, axis), dim)


def gathered_by_axis(value, axes, dim):
    if not axes:
        return value
    nearer = lax.all_gather(value, axes[-1], axis=dim, tiled=True)
    return gathered_by_axis(nearer, axes[:-1], dim)


def sum_by_axis(value, axes, dim):
    if not axes:
        return value
    nearer = lax.psum_scatter(value, axes[0], scatter_dimension=dim, tiled=True)
    return sum_by_axis(nearer, axes[1:], dim)


def cut_along(value, dim, size):
    shape = value.shape
    pieces = value.reshape(*shape[:dim], size, shape[dim] // size, *shape[dim + 1 :])
    return jnp.moveaxis(pieces, dim, 0)


def summed_on_arrival(value, axis, dim):
    size = lax.axis_size(axis)
    pieces = lax.all_to_all(cut_along(value, dim, size), axis, 0, 0, tiled=True)
    return jnp.sum(pieces.astype(jnp.float32), axis=0)


def silu_terms(preact):
    sigma = jax.nn.sigmoid(preact)
    slope = sigma * (1.0 + preact * (1.0 - sigma))
    curvature = sigma * (1.0 - sigma) * (2.0 + preact * (1.0 - 2.0 * sigma))
    return (preact * sigma, slope, curvature)


def contracted_array(form, left, right):
    return jnp.einsum(form, left, right, preferred_element_type=jnp.float32)


def transposed(left, right):
    return lax.dot_general(
        left, right, (((1,), (1,)), ((), ())), preferred_element_type=jnp.float32
    )


def local(
    inputs,
    probe_projector,
    address_projector,
    payload_projector,
    checkpoints,
    out_grad,
    adjoint,
    inner_rate,
):
    spans = inputs.shape[0]
    tokens = inputs.shape[1]
    head_count = inner_rate.shape[0]
    head_size = probe_projector.shape[1] // head_count
    factor = (inner_rate / (tokens * lax.axis_size(TOK)))[None, :, None]
    field_indices = gathered_copies(inputs, "head", 2)
    first_addend = contracted_array("knw,we->kne", field_indices, probe_projector)
    central_addend = contracted_array("knw,we->kne", field_indices, address_projector)
    final_addend = contracted_array("knw,we->kne", field_indices, payload_projector)
    query_all = first_addend.astype(jnp.bfloat16)
    keys_all = central_addend.astype(jnp.bfloat16)
    values_all = final_addend.astype(jnp.bfloat16)
    adjoint_now = adjoint
    outputs = []
    for span in reversed(range(spans)):
        weights = gathered_copies(checkpoints[span], TOK, 2)
        adjoint_bf = gathered_by_axis(adjoint_now.astype(jnp.bfloat16), TOK, 2)
        first_weight = weights[0]
        third_weight = weights[1]
        second_weight = weights[2]
        queries = query_all[span].reshape(tokens, head_count, head_size)
        keys_now = keys_all[span].reshape(tokens, head_count, head_size)
        values = values_all[span].reshape(tokens, head_count, head_size)
        grad_now = out_grad[span].reshape(tokens, head_count, head_size)
        ahead = "nhd,hdf->nhf"
        gate_query = contracted_array(ahead, queries, first_weight)
        lift_query = contracted_array(ahead, queries, third_weight)
        back_query = contracted_array(ahead, grad_now, second_weight)
        gate_keys = contracted_array(ahead, keys_now, first_weight)
        lift_keys = contracted_array(ahead, keys_now, third_weight)
        echo_values = contracted_array(ahead, values, second_weight)
        pull_values = contracted_array(ahead, values, adjoint_bf[2])
        side_one = contracted_array(ahead, keys_now, adjoint_bf[0])
        side_three = contracted_array(ahead, keys_now, adjoint_bf[1])
        swish_query, slope_query, unused = silu_terms(gate_query)
        swish_keys, slope_keys, bend_keys = silu_terms(gate_keys)
        hidden_act = (swish_query * lift_query).astype(jnp.bfloat16)
        gate_back = (back_query * lift_query * slope_query).astype(jnp.bfloat16)
        lift_back = (back_query * swish_query).astype(jnp.bfloat16)
        gate_second = (
            factor
            * (
                slope_keys * lift_keys * pull_values
                + side_one * echo_values * lift_keys * bend_keys
                + side_three * echo_values * slope_keys
            )
        ).astype(jnp.bfloat16)
        lift_second = (
            factor * (swish_keys * pull_values + side_one * echo_values * slope_keys)
        ).astype(jnp.bfloat16)
        down_second = (
            factor * (side_one * lift_keys * slope_keys + side_three * swish_keys)
        ).astype(jnp.bfloat16)
        pull_second = (factor * swish_keys * lift_keys).astype(jnp.bfloat16)
        side_first = (factor * echo_values * lift_keys * slope_keys).astype(jnp.bfloat16)
        side_third = (factor * echo_values * swish_keys).astype(jnp.bfloat16)
        if span > 0:
            outer = "nhd,nhf->hdf"
            both_rows = jnp.concatenate([keys_now, queries], axis=0)
            own_terms = jnp.stack(
                [
                    contracted_array(
                        outer, both_rows, jnp.concatenate([gate_second, gate_back], axis=0)
                    ),
                    contracted_array(
                        outer, both_rows, jnp.concatenate([lift_second, lift_back], axis=0)
                    ),
                    contracted_array(
                        outer,
                        jnp.concatenate([values, grad_now], axis=0),
                        jnp.concatenate([down_second, hidden_act], axis=0),
                    ),
                ]
            )
            adjoint_now = adjoint_now + sum_by_axis(own_terms, TOK, 2)
        behind = "nhf,hdf->nhd"
        query_grad = (
            contracted_array(behind, gate_back, first_weight)
            + contracted_array(behind, lift_back, third_weight)
        ).astype(jnp.bfloat16)
        keys_grad = (
            contracted_array(behind, gate_second, first_weight)
            + contracted_array(behind, lift_second, third_weight)
            + contracted_array(behind, side_first, adjoint_bf[0])
            + contracted_array(behind, side_third, adjoint_bf[1])
        ).astype(jnp.bfloat16)
        values_grad = (
            contracted_array(behind, down_second, second_weight)
            + contracted_array(behind, pull_second, adjoint_bf[2])
        ).astype(jnp.bfloat16)
        partial_value = transposed(query_grad.reshape(tokens, -1), probe_projector)
        partial_value = partial_value + transposed(keys_grad.reshape(tokens, -1), address_projector)
        partial_value = partial_value + transposed(
            values_grad.reshape(tokens, -1), payload_projector
        )
        outputs.append(
            summed_on_arrival(partial_value.astype(jnp.bfloat16), "head", 1).astype(jnp.bfloat16)
        )
    return jnp.stack(outputs[::-1])


def solution(mesh):
    split = Mesh(mesh.devices.reshape(16, 4, mesh.shape["head"]), ("tok_0", "tok_1", "head"))
    placed = (
        P(None, TOK, "head"),
        P(None, "head"),
        P(None, "head"),
        P(None, "head"),
        P(None, None, "head", TOK, None),
        P(None, TOK, "head"),
        P(None, "head", TOK, None),
        P("head"),
    )
    return jax.shard_map(
        local, mesh=split, in_specs=placed, out_specs=P(None, TOK, "head"), check_vma=False
    )
```

profile of v0, /device:TPU:1, one launch (start us, length us, event | category | flops | bytes accessed | tf_op | source)
XLA Modules:
  0.0 374.7 jit_solution(9380460741426993121)
XLA Ops:
  6.5 2.6 broadcast_in_dim.11
  9.1 10.5 %all-to-all-start.1 = ((bf16[8,2,256,256]{3,2,1,0:T(8,128)(2,1)}), bf16[8,2,256,256]{3,2,1,0:T(8,128)(2,1)S(1)}, u32[]{:S(2)}, u32[]{:S(2)}) async-start(bf16[8,2,256,256]{3,2,1,0:T(8,128)(2,1)} %broadcast_in_dim.11), calls=%async_computation.1 | async-start | bytes 4194304 | tf_op jit(solution)/shard_map/all_to_all | solution.py:18
  19.6 26.2 %all-to-all-done.1 = bf16[8,2,256,256]{3,2,1,0:T(8,128)(2,1)S(1)} async-done(((bf16[8,2,256,256]{3,2,1,0:T(8,128)(2,1)}), bf16[8,2,256,256]{3,2,1,0:T(8,128)(2,1)S(1)}, u32[]{:S(2)}, u32[]{:S(2)}) %all-to-all-start.1) | async-done | bytes 2097184 | tf_op jit(solution)/shard_map/all_to_all | solution.py:18
  45.8 1.1 broadcast_in_dim.12
  46.9 14.1 %all-to-all-start.2 = ((bf16[64,3,1,4,512]{4,3,2,1,0:T(4,128)(2,1)}), bf16[64,3,1,4,512]{4,3,2,1,0:T(4,128)(2,1)}, u32[]{:S(2)}, u32[]{:S(2)}) async-start(bf16[64,3,1,4,512]{4,3,2,1,0:T(4,128)(2,1)} %broadcast_in_dim.12), calls=%async_computation.2 | async-start | bytes 1572864 | tf_op jit(solution)/shard_map/all_to_all | solution.py:18
  61.1 9.8 %all_gather.12 = bf16[3,1,16,512]{3,0,1,2:T(4,128)(2,1)S(1)} all-gather(bf16[3,1,4,512]{3,0,1,2:T(4,128)(2,1)S(1)} %copy.79), channel_id=1, replica_groups=mesh['tok_0'=16,'tok_1'=4,'head'=8] {'tok_1'}, dimensions={2}, use_global_device_ids=true | all-gather | bytes 61440 | tf_op jit(solution)/shard_map/all_gather | solution.py:28
  71.6 1.3 dynamic-slice
  73.5 45.8 %all_gather.13 = bf16[3,1,256,512]{3,2,1,0:T(8,128)(2,1)S(1)} all-gather(bf16[3,1,16,512]{3,2,1,0:T(8,128)(2,1)S(1)} %copy.80), channel_id=1, replica_groups=mesh['tok_0'=16,'tok_1'=4,'head'=8] {'tok_0'}, dimensions={2}, use_global_device_ids=true | all-gather | bytes 835584 | tf_op jit(solution)/shard_map/all_gather | solution.py:28
  119.6 1.2 copy-done.6
  121.6 1.1 convolution_bitcast_fusion.12
  123.4 1.1 convolution_bitcast_fusion.13
  125.9 0.7 slice_bitcast_fusion.32
  126.7 1.1 broadcast_in_dim.10
  127.8 13.2 %all-to-all-start = ((bf16[64,3,1,4,512]{4,3,2,1,0:T(4,128)(2,1)}), bf16[64,3,1,4,512]{4,3,2,1,0:T(4,128)(2,1)}, u32[]{:S(2)}, u32[]{:S(2)}) async-start(bf16[64,3,1,4,512]{4,3,2,1,0:T(4,128)(2,1)} %broadcast_in_dim.10), calls=%async_computation | async-start | bytes 1572864 | tf_op jit(solution)/shard_map/all_to_all | solution.py:18
  141.2 1.4 fusion.146
  142.7 1.1 convolution_bitcast_fusion.7
  144.1 1.1 convolution_bitcast_fusion.9
  145.6 1.9 multiply_convert_fusion.8
  147.8 0.8 multiply_convert_fusion.9
  150.1 1.3 pad_maximum_fusion
  151.4 2.0 fusion.79
  153.5 1.2 fusion.75
  154.7 1.9 fusion.72
  156.9 1.1 convolution_add_fusion.6
  158.1 3.1 fusion.15
  161.1 3.2 convolution_add_fusion.1
  164.3 3.5 fusion.1
  167.8 2.3 copy.120
  170.1 8.0 %all-to-all-done = bf16[64,3,1,4,512]{4,3,2,1,0:T(4,128)(2,1)} async-done(((bf16[64,3,1,4,512]{4,3,2,1,0:T(4,128)(2,1)}), bf16[64,3,1,4,512]{4,3,2,1,0:T(4,128)(2,1)}, u32[]{:S(2)}, u32[]{:S(2)}) %all-to-all-start) | async-done | bytes 786464 | tf_op jit(solution)/shard_map/all_to_all | solution.py:18
  178.1 11.7 %all-to-all-start.4 = ((bf16[8,256,256]{2,1,0:T(8,128)(2,1)}), bf16[8,256,256]{2,1,0:T(8,128)(2,1)}, u32[]{:S(2)}, u32[]{:S(2)}) async-start(bf16[8,256,256]{2,1,0:T(8,128)(2,1)} %bitcast.365), calls=%async_computation.5 | async-start | bytes 2097152 | tf_op jit(solution)/shard_map/all_to_all | solution.py:47
  189.7 1.4 fusion.145
  191.4 1.2 convolution_bitcast_fusion.18
  192.8 1.1 convolution_bitcast_fusion.1
  194.0 2.0 convolution_bitcast_fusion.20
  195.9 2.4 fusion.20
  198.3 3.3 fusion.16
  201.6 19.2 %reduce-scatter.3.cloned.1.call-done = f32[3,1,16,512]{3,2,1,0:T(8,128)} async-done(((f32[3,1,256,512]{3,2,1,0:T(8,128)}), f32[3,1,16,512]{3,2,1,0:T(8,128)}) %reduce-scatter.3.cloned.1.call-update) | async-done | bytes 98320 | tf_op jit(solution)/shard_map/reduce_scatter | solution.py:35
  221.1 63.2 %all-reduce.3.cloned.1.call-done = f32[3,1,16,512]{3,2,1,0:T(8,128)} async-done(((f32[3,1,16,512]{3,2,1,0:T(8,128)}), f32[3,1,16,512]{3,2,1,0:T(8,128)}) %all-reduce.3.cloned.1.call-update) | async-done | bytes 98320
  284.3 0.8 fusion.121
  285.1 9.0 %all_gather.14 = bf16[3,1,16,512]{3,0,1,2:T(4,128)(2,1)S(1)} all-gather(bf16[3,1,4,512]{3,0,1,2:T(4,128)(2,1)S(1)} %copy.88), channel_id=1, replica_groups=mesh['tok_0'=16,'tok_1'=4,'head'=8] {'tok_1'}, dimensions={2}, use_global_device_ids=true | all-gather | bytes 61440 | tf_op jit(solution)/shard_map/all_gather | solution.py:28
  294.1 29.0 %all_gather.15 = bf16[3,1,256,512]{3,2,1,0:T(8,128)(2,1)S(1)} all-gather(bf16[3,1,16,512]{3,2,1,0:T(8,128)(2,1)S(1)} %copy.89), channel_id=1, replica_groups=mesh['tok_0'=16,'tok_1'=4,'head'=8] {'tok_0'}, dimensions={2}, use_global_device_ids=true | all-gather | bytes 835584 | tf_op jit(solution)/shard_map/all_gather | solution.py:28
  325.9 1.1 convolution_add_fusion.11
  327.0 3.2 convolution_add_fusion.3
  330.2 3.4 fusion
  333.6 2.3 copy.121
  335.9 16.1 %all-to-all-start.3 = ((bf16[8,256,256]{2,1,0:T(8,128)(2,1)}), bf16[8,256,256]{2,1,0:T(8,128)(2,1)S(1)}, u32[]{:S(2)}, u32[]{:S(2)}) async-start(bf16[8,256,256]{2,1,0:T(8,128)(2,1)} %bitcast.367), calls=%async_computation.4 | async-start | bytes 2097152 | tf_op jit(solution)/shard_map/all_to_all | solution.py:47
  352.0 1.4 reduce_sum.25
  353.4 13.6 %all-to-all-done.3 = bf16[8,256,256]{2,1,0:T(8,128)(2,1)S(1)} async-done(((bf16[8,256,256]{2,1,0:T(8,128)(2,1)}), bf16[8,256,256]{2,1,0:T(8,128)(2,1)S(1)}, u32[]{:S(2)}, u32[]{:S(2)}) %all-to-all-start.3) | async-done | bytes 1048608 | tf_op jit(solution)/shard_map/all_to_all | solution.py:47
  (107 shorter events, 10.5 us)
Async XLA Ops:
  6.5 118.6 %copy-start = (bf16[2048,256]{1,0:T(8,128)(2,1)S(1)}, bf16[2048,256]{1,0:T(8,128)(2,1)}, u32[]{:S(2)}) copy-start(bf16[2048,256]{1,0:T(8,128)(2,1)} %param.9) | copy-start | bytes 3145732
  9.1 10.5 %copy-start.33 = (bf16[2,3,1,4,512]{4,3,2,1,0:T(4,128)(2,1)S(1)}, bf16[2,3,1,4,512]{4,3,2,1,0:T(4,128)(2,1)}, u32[]{:S(2)}) copy-start(bf16[2,3,1,4,512]{4,3,2,1,0:T(4,128)(2,1)} %param.12) | copy-start | bytes 73732
  9.1 36.7 %all-to-all-start.1 = ((bf16[8,2,256,256]{3,2,1,0:T(8,128)(2,1)}), bf16[8,2,256,256]{3,2,1,0:T(8,128)(2,1)S(1)}, u32[]{:S(2)}, u32[]{:S(2)}) async-start(bf16[8,2,256,256]{3,2,1,0:T(8,128)(2,1)} %broadcast_in_dim.11), calls=%async_computation.1 | async-start | bytes 4194304 | tf_op jit(solution)/shard_map/all_to_all | solution.py:18
  19.6 41.4 %copy-start.31 = (f32[3,1,4,512]{3,2,1,0:T(4,128)S(1)}, f32[3,1,4,512]{3,2,1,0:T(4,128)}, u32[]{:S(2)}) copy-start(f32[3,1,4,512]{3,2,1,0:T(4,128)} %param.14) | copy-start | bytes 73732
  46.9 79.7 %all-to-all-start.2 = ((bf16[64,3,1,4,512]{4,3,2,1,0:T(4,128)(2,1)}), bf16[64,3,1,4,512]{4,3,2,1,0:T(4,128)(2,1)}, u32[]{:S(2)}, u32[]{:S(2)}) async-start(bf16[64,3,1,4,512]{4,3,2,1,0:T(4,128)(2,1)} %broadcast_in_dim.12), calls=%async_computation.2 | async-start | bytes 1572864 | tf_op jit(solution)/shard_map/all_to_all | solution.py:18
  119.3 4.0 %copy-start.4 = (bf16[3,1,256,512]{3,2,1,0:T(8,128)(2,1)}, bf16[3,1,256,512]{3,2,1,0:T(8,128)(2,1)S(1)}, u32[]{:S(2)}) copy-start(bf16[3,1,256,512]{3,2,1,0:T(8,128)(2,1)S(1)} %all_gather.13) | copy-start | bytes 2359300
  119.3 1.5 copy-start.6
  120.9 1.8 copy-start.7
  122.7 1.8 copy-start.18
  123.4 2.5 copy-start.14
  125.9 16.8 %copy-start.19 = (bf16[2,256,256]{2,1,0:T(8,128)(2,1)}, bf16[2,256,256]{2,1,0:T(8,128)(2,1)S(1)}, u32[]{:S(2)}) copy-start(bf16[2,256,256]{2,1,0:T(8,128)(2,1)S(1)} %convolution_convert_fusion.2) | copy-start | bytes 786436
  127.8 50.3 %all-to-all-start = ((bf16[64,3,1,4,512]{4,3,2,1,0:T(4,128)(2,1)}), bf16[64,3,1,4,512]{4,3,2,1,0:T(4,128)(2,1)}, u32[]{:S(2)}, u32[]{:S(2)}) async-start(bf16[64,3,1,4,512]{4,3,2,1,0:T(4,128)(2,1)} %broadcast_in_dim.10), calls=%async_computation | async-start | bytes 1572864 | tf_op jit(solution)/shard_map/all_to_all | solution.py:18
  141.0 79.8 %reduce-scatter.3.cloned.1.call-start = ((), (), s32[]{:S(2)}) async-start(), calls=%async_computation.6 | async-start | bytes 1671168 | tf_op jit(solution)/shard_map/reduce_scatter | solution.py:35
  144.0 12.9 %copy-start.2 = (f32[256,1,512]{0,2,1:T(8,128)}, f32[256,1,512]{0,2,1:T(8,128)S(1)}, u32[]{:S(2)}) copy-start(f32[256,1,512]{0,2,1:T(8,128)S(1)} %convolution_bitcast_fusion.15) | copy-start | bytes 1572868
  145.3 2.2 copy-start.15
  145.5 2.2 copy-start.8
  145.6 2.2 copy-start.5
  145.6 2.2 copy-start.20
  145.6 2.2 copy-start.21
  147.5 1.2 copy-start.27
  147.5 1.8 copy-start.22
  147.8 0.8 copy-start.12
  147.8 1.0 copy-start.29
  147.8 1.1 copy-start.30
  148.6 1.5 copy-start.23
  148.6 1.5 copy-start.24
  148.6 1.5 copy-start.25
  148.6 1.1 copy-start.28
  151.4 5.2 %copy-start.26 = (bf16[256,1,512]{0,2,1:T(8,128)(2,1)S(1)}, bf16[256,1,512]{0,2,1:T(8,128)(2,1)}, u32[]{:S(2)}) copy-start(bf16[256,1,512]{0,2,1:T(8,128)(2,1)} %copy-done.25) | copy-start | bytes 786436
  151.4 5.5 %copy-start.9 = (f32[256,1,512]{0,2,1:T(8,128)S(1)}, f32[256,1,512]{0,2,1:T(8,128)}, u32[]{:S(2)}) copy-start(f32[256,1,512]{0,2,1:T(8,128)} %copy-done.8) | copy-start | bytes 1572868
  151.4 5.5 %copy-start.13 = (f32[256,1,512]{0,2,1:T(8,128)S(1)}, f32[256,1,512]{0,2,1:T(8,128)}, u32[]{:S(2)}) copy-start(f32[256,1,512]{0,2,1:T(8,128)} %copy-done.12) | copy-start | bytes 1572868
  156.6 1.4 copy-start.17
  178.1 157.8 %all-to-all-start.4 = ((bf16[8,256,256]{2,1,0:T(8,128)(2,1)}), bf16[8,256,256]{2,1,0:T(8,128)(2,1)}, u32[]{:S(2)}, u32[]{:S(2)}) async-start(bf16[8,256,256]{2,1,0:T(8,128)(2,1)} %bitcast.365), calls=%async_computation.5 | async-start | bytes 2097152 | tf_op jit(solution)/shard_map/all_to_all | solution.py:47
  189.7 94.6 %all-reduce.3.cloned.1.call-start = ((), (), s32[]{:S(2)}) async-start(), calls=%async_computation.7 | async-start | bytes 196608
  191.1 1.7 copy-start.16
  192.8 133.0 %copy-start.3 = (f32[256,1,512]{0,2,1:T(8,128)}, f32[256,1,512]{0,2,1:T(8,128)S(1)}, u32[]{:S(2)}) copy-start(f32[256,1,512]{0,2,1:T(8,128)S(1)} %convolution_bitcast_fusion.17) | copy-start | bytes 1572868
  198.3 86.0 %copy-start.32 = (f32[3,1,4,512]{3,2,1,0:T(4,128)S(1)}, f32[3,1,4,512]{3,2,1,0:T(4,128)}, u32[]{:S(2)}) copy-start(f32[3,1,4,512]{3,2,1,0:T(4,128)} %param.14) | copy-start | bytes 73732
  221.1 104.8 %copy-start.10 = (f32[256,1,512]{0,2,1:T(8,128)}, f32[256,1,512]{0,2,1:T(8,128)S(1)}, u32[]{:S(2)}) copy-start(f32[256,1,512]{0,2,1:T(8,128)S(1)} %convolution_bitcast_fusion.16) | copy-start | bytes 1572868
  323.2 2.7 copy-start.1
  323.7 1.0 copy-start.11
  335.9 31.1 %all-to-all-start.3 = ((bf16[8,256,256]{2,1,0:T(8,128)(2,1)}), bf16[8,256,256]{2,1,0:T(8,128)(2,1)S(1)}, u32[]{:S(2)}, u32[]{:S(2)}) async-start(bf16[8,256,256]{2,1,0:T(8,128)(2,1)} %bitcast.367), calls=%async_computation.4 | async-start | bytes 2097152 | tf_op jit(solution)/shard_map/all_to_all | solution.py:47
Sparse Core Ops, SparseCore 0:
  151.5 69.1 reduce-scatter.2
  223.1 61.1 all-reduce.2
where the time goes:
time: 376 us; the launch traced here: 375 us
  waiting for transfers between devices  130 us (35%)
  blocking collectives  93.7 us (25%)
  starting transfers between devices  65.8 us (18%)
  matrix products  47.7 us (13%)
  local copies, waits for them, and re-layouts  17.6 us (5%)
  between operations  15.3 us (4%)
  other arithmetic  4.34 us (1%)
    all_gather x4, blocking collectives, gathered_by_axis(): nearer = lax.all_gather(value, axes[-1], axis=dim, tiled=True)  93.7 us
    unnamed x3, waiting for transfers between devices  63.3 us
    all_to_all x3, starting transfers between devices, copy_for_each(): return lax.all_to_all(copies, axis, split_axis=0, concat_axis=0, tiled=True)  37.8 us
    all_to_all x3, waiting for transfers between devices, copy_for_each(): return lax.all_to_all(copies, axis, split_axis=0, concat_axis=0, tiled=True)  34.2 us
    dot_general x33, matrix products, contracted_array(): return jnp.einsum(form, left, right, preferred_element_type=jnp.float32)  28.2 us
    all_to_all x2, starting transfers between devices, summed_on_arrival(): pieces = lax.all_to_all(cut_along(value, dim, size), axis, 0, 0, tiled=True)  27.8 us
    dot_general x6, matrix products, transposed(): lax.dot_general(left, right, (((1,), (1,)), ((), ())), preferred_element_...  19.5 us
    reduce_scatter x1, waiting for transfers between devices, sum_by_axis(): nearer = lax.psum_scatter(value, axes[0], scatter_dimension=dim, tiled=True)  19.2 us
  transfers between devices with their start and end apart: 7, of which 5 were waited for; matrix products, arithmetic and copies ran while one was open for 17% of the time, Pallas kernels for 0%

commit v1 on v0

v1 whole, which is shorter than its diff:
```python
import jax
import jax.numpy as jnp
from jax import lax
from jax.experimental import pallas as pl
from jax.experimental.pallas import tpu as pltpu
from jax.sharding import Mesh
from jax.sharding import PartitionSpec as P

AXES = ("z", "y", "x", "c")
NZ, NY, NX, NC = 16, 4, 4, 2
MESH = pl.DeviceIdType.MESH
BF = jnp.bfloat16
F32 = jnp.float32
T = 256
DH = 256
F = 512
D = 2048
W_LATE, B_LATE, W_EARLY, B_EARLY = 0, 1, 2, 3


def mm(a, b):
    return jnp.dot(a, b, preferred_element_type=F32)


def mm_t(a, b):
    return lax.dot_general(a, b, (((1,), (1,)), ((), ())), preferred_element_type=F32)


def t_mm(a, b):
    return lax.dot_general(a, b, (((0,), (0,)), ((), ())), preferred_element_type=F32)


def native_row(position, near_first):
    high, middle = position // 64, (position // 16) % 4
    y, low = (middle, high) if near_first else (high, middle)
    return 64 * ((position // 4) % 4) + 16 * low + 4 * y + position % 4


def permutation(near_first):
    row = lax.broadcasted_iota(jnp.int32, (DH, DH), 0)
    position = lax.broadcasted_iota(jnp.int32, (DH, DH), 1)
    return jnp.where(row == native_row(position, near_first), 1.0, 0.0).astype(BF)


def kernel(
    xin, pq, pk, pv, ck, og, adj, rate, out,
    xg, pc, pp, gath, fb, tile, qkv, o_s, fw, hb, own, rsend,
    ry, acc1, s1, rn, rn2, acc2, s2, ry2, fs, fsf, rf, gcat, gp, pb, ro,
    xs, xr, fas, far, nas, nar, yas, yar, nbs, nbr, ybs, ybr,
    rys, ryr, rns, rnr, rn2s, rn2r, ry2s, ry2r, rfs, rfr, cs, cr, hs, hr,
):
    z, y = lax.axis_index("z"), lax.axis_index("y")
    x, c = lax.axis_index("x"), lax.axis_index("c")

    def dev(dz=0, dy=0, dx=0, dc=0):
        return (
            lax.rem(z + dz + NZ, NZ), lax.rem(y + dy, NY), lax.rem(x + dx, NX), lax.rem(c + dc, NC)
        )

    zh, zl = z // 4, lax.rem(z, 4)
    skip = 4 * c - 2
    near = [1, -1, skip]
    fars = [4, -4, 8]

    barrier = pltpu.get_barrier_semaphore()
    partners = [dev(dz=d) for d in (1, -1, 2, -2, 4, -4, 8)]
    partners += [dev(dy=d) for d in (1, 2, 3)] + [dev(dx=d) for d in (1, 2, 3)] + [dev(dc=1)]
    for partner in partners:
        pl.semaphore_signal(barrier, inc=1, device_id=partner, device_id_type=MESH)

    started = []

    def send(src, dst, ssem, rsem, device):
        copy = pltpu.make_async_remote_copy(
            src_ref=src, dst_ref=dst, send_sem=ssem, recv_sem=rsem,
            device_id=device, device_id_type=MESH,
        )
        copy.start()
        started.append(copy)
        return copy

    fb[W_LATE, zh] = ck[1]
    fb[W_EARLY, zh] = ck[0]
    fb[B_LATE, zh] = adj[...].astype(BF)
    column = pl.multiple_of((x * 2 + c) * DH, DH)
    for s in range(2):
        xg[s, :, pl.ds(column, DH)] = xin[s]

    pl.semaphore_wait(barrier, len(partners))

    far_copies = {}

    def far_send(s):
        far_copies[s] = [
            send(fb.at[s, zh], fb.at[s, zh], fas.at[s, i], far.at[s, i], dev(dz=d))
            for i, d in enumerate(fars)
        ]

    x_copies = {}

    def x_send(s):
        block = xg.at[s, :, pl.ds(column, DH)]
        x_copies[s] = [
            send(xin.at[s], block, xs.at[s, i], xr.at[s, i], dev(dx=i + 1)) for i in range(3)
        ]
        x_copies[s].append(send(xin.at[s], block, xs.at[s, 3], xr.at[s, 3], dev(dc=1)))

    far_send(W_LATE)
    far_send(B_LATE)
    x_send(1)
    x_send(0)
    far_send(W_EARLY)

    plain, swapped = permutation(False), permutation(True)
    for i, (ref, order) in enumerate(((pq, plain), (pk, plain), (pv, swapped))):
        for j in range(8):
            rows = pl.ds(j * DH, DH)
            pc[rows, pl.ds(i * DH, DH)] = mm(ref[rows, :], order).astype(BF)
    for s in range(2):
        o_s[s] = mm(og[s], swapped).astype(BF)

    other = 1 - c
    pc_copies = []
    for i in range(4):
        rows = pl.multiple_of((i * 2 + other) * DH, DH)
        pc_copies.append(
            send(pc.at[pl.ds(rows, DH), :], pp.at[i], cs.at[i], cr.at[i], dev(dc=1))
        )

    blocks01 = pl.multiple_of(y * 64 + zl * 16, 16)
    blocks2 = pl.multiple_of(zl * 64 + y * 16, 16)
    near_a, y_a, y_b, near_b = {}, {}, {}, {}

    def gather_far(s):
        for copy in far_copies[s]:
            copy.wait_recv()
        for m in range(3):
            for k in range(4):
                tile[m, pl.ds(4 * k, 4), :] = fb[s, k, m].astype(F32)
        gath[s, 0, pl.ds(blocks01, 16), :] = tile[0].astype(BF)
        gath[s, 1, pl.ds(blocks01, 16), :] = tile[1].astype(BF)
        gath[s, 2, pl.ds(blocks2, 16), :] = tile[2].astype(BF)
        first = gath.at[s, pl.ds(0, 2), pl.ds(blocks01, 16), :]
        second = gath.at[s, 2, pl.ds(blocks2, 16), :]
        near_a[s] = [
            send(first, first, nas.at[s, i], nar.at[s, i], dev(dz=d)) for i, d in enumerate(near)
        ]
        y_b[s] = [
            send(second, second, ybs.at[s, i], ybr.at[s, i], dev(dy=i + 1)) for i in range(3)
        ]

    def gather_middle(s):
        for copy in near_a[s]:
            copy.wait_recv()
        first = gath.at[s, pl.ds(0, 2), pl.ds(pl.multiple_of(y * 64, 64), 64), :]
        y_a[s] = [
            send(first, first, yas.at[s, i], yar.at[s, i], dev(dy=i + 1)) for i in range(3)
        ]
        for copy in y_b[s]:
            copy.wait_recv()
        second = gath.at[s, 2, pl.ds(pl.multiple_of(zl * 64, 64), 64), :]
        near_b[s] = [
            send(second, second, nbs.at[s, i], nbr.at[s, i], dev(dz=d)) for i, d in enumerate(near)
        ]

    def gather_end(s):
        for copy in y_a[s] + near_b[s]:
            copy.wait_recv()

    relays = {}

    def x_relay(s):
        relays[s] = []
        for i in range(3):
            x_copies[s][i].wait_recv()
            source = pl.multiple_of((lax.rem(x + 3 - i, NX) * 2 + c) * DH, DH)
            block = xg.at[s, :, pl.ds(source, DH)]
            relays[s].append(send(block, block, xs.at[s, 4 + i], xr.at[s, 4 + i], dev(dc=1)))

    def project(s):
        for copy in [x_copies[s][3]] + relays[s]:
            copy.wait_recv()
        for i in range(3):
            qkv[s, i] = mm(xg[s], pc[:, pl.ds(i * DH, DH)]).astype(BF)

    factor = rate[0] / 16384.0

    def forward(s, w):
        q, k, v = qkv[s, 0], qkv[s, 1], qkv[s, 2]
        fw[s, 0] = mm(q, gath[w, 0])
        fw[s, 1] = mm(q, gath[w, 1])
        fw[s, 2] = mm(o_s[s], gath[w, 2])
        fw[s, 3] = mm(k, gath[w, 0])
        fw[s, 4] = mm(k, gath[w, 1])
        fw[s, 5] = mm(v, gath[w, 2])

        @pl.loop(0, T // 16)
        def _(step):
            rows = pl.ds(pl.multiple_of(step * 16, 16), 16)
            gate, lift, back = fw[s, 0, rows, :], fw[s, 1, rows, :], fw[s, 2, rows, :]
            g = jax.nn.sigmoid(gate)
            act = gate * g
            if s > 0:
                hb[s, 0, rows, :] = (act * lift).astype(BF)
            hb[s, 1, rows, :] = (back * lift * (g * (1.0 + gate * (1.0 - g)))).astype(BF)
            hb[s, 2, rows, :] = (back * act).astype(BF)
            gate, u, e = fw[s, 3, rows, :], fw[s, 4, rows, :], fw[s, 5, rows, :]
            g = jax.nn.sigmoid(gate)
            act = factor * gate * g
            slope = factor * (g * (1.0 + gate * (1.0 - g)))
            bend = factor * (g * (1.0 - g) * (2.0 + gate * (1.0 - 2.0 * g)))
            us = u * slope
            fw[s, 0, rows, :] = us
            fw[s, 1, rows, :] = e * u * bend
            fw[s, 2, rows, :] = e * slope
            fw[s, 3, rows, :] = act
            hb[s, 6, rows, :] = (act * u).astype(BF)
            hb[s, 7, rows, :] = (e * us).astype(BF)
            hb[s, 8, rows, :] = (e * act).astype(BF)

    def second(s, b):
        fw[s, 6] = mm(qkv[s, 2], gath[b, 2])
        fw[s, 7] = mm(qkv[s, 1], gath[b, 0])
        fw[s, 8] = mm(qkv[s, 1], gath[b, 1])

        @pl.loop(0, T // 16)
        def _(step):
            rows = pl.ds(pl.multiple_of(step * 16, 16), 16)
            pull, one, three = fw[s, 6, rows, :], fw[s, 7, rows, :], fw[s, 8, rows, :]
            us, eub, es, act = (fw[s, i, rows, :] for i in range(4))
            hb[s, 3, rows, :] = (us * pull + one * eub + three * es).astype(BF)
            hb[s, 4, rows, :] = (act * pull + one * es).astype(BF)
            hb[s, 5, rows, :] = (one * us + three * act).astype(BF)

    def back_queries(s, w):
        grad = mm_t(hb[s, 1], gath[w, 0]) + mm_t(hb[s, 2], gath[w, 1])
        gcat[s, :, pl.ds(0, DH)] = grad.astype(BF)

    def back_rest(s, w, b):
        grad = mm_t(hb[s, 3], gath[w, 0]) + mm_t(hb[s, 4], gath[w, 1])
        grad = grad + mm_t(hb[s, 7], gath[b, 0]) + mm_t(hb[s, 8], gath[b, 1])
        gcat[s, :, pl.ds(DH, DH)] = grad.astype(BF)
        grad = mm_t(hb[s, 5], gath[w, 2]) + mm_t(hb[s, 6], gath[b, 2])
        gcat[s, :, pl.ds(2 * DH, DH)] = grad.astype(BF)

    pair = {}

    def exchange(s):
        pair[s] = send(gcat.at[s], gp.at[s], cs.at[4 + s], cr.at[4 + s], dev(dc=1))

    heads = {}

    def partial_of(s, step):
        to = lax.rem(x + step, NX)
        rows = pl.multiple_of((to * 2 + c) * DH, DH)
        return mm_t(gcat[s], pc[pl.ds(rows, DH), :]) + mm_t(gp[s], pp[to])

    def heads_send(s):
        if s == 1:
            for copy in pc_copies:
                copy.wait_recv()
        pair[s].wait_recv()
        heads[s] = []
        for i, step in enumerate((2, 1, 3)):
            pb[s, i] = partial_of(s, step).astype(BF)
            heads[s].append(
                send(pb.at[s, i], ro.at[s, i], hs.at[s, i], hr.at[s, i], dev(dx=step))
            )

    def heads_end(s):
        total = partial_of(s, 0)
        for i in range(3):
            heads[s][i].wait_recv()
            total = total + ro[s, i].astype(F32)
        out[s] = total.astype(BF)

    gather_far(W_LATE)
    gather_far(B_LATE)
    x_relay(1)
    gather_middle(W_LATE)
    gather_middle(B_LATE)
    gather_far(W_EARLY)
    project(1)
    gather_end(W_LATE)
    forward(1, W_LATE)
    gather_middle(W_EARLY)
    gather_end(B_LATE)
    second(1, B_LATE)

    q, k, v = qkv[1, 0], qkv[1, 1], qkv[1, 2]
    ry_copies = []
    for m in range(2):
        own[m] = t_mm(k, hb[1, 3 + m]) + t_mm(q, hb[1, 1 + m])
        rsend[m] = own[m].astype(BF)
        for i in range(3):
            rows = pl.multiple_of(lax.rem(y + i + 1, NY) * 64, 64)
            ry_copies.append(
                send(rsend.at[m, pl.ds(rows, 64), :], ry.at[m, i], rys.at[m, i], ryr.at[m, i],
                     dev(dy=i + 1))
            )
    own[2] = t_mm(v, hb[1, 5]) + t_mm(o_s[1], hb[1, 0])
    rsend[2] = own[2].astype(BF)
    rn2_copies = []
    for i, d in enumerate(near):
        rows = pl.multiple_of(lax.rem(z + d + NZ, 4) * 64, 64)
        rn2_copies.append(
            send(rsend.at[2, pl.ds(rows, 64), :], rn2.at[i], rn2s.at[i], rn2r.at[i], dev(dz=d))
        )

    back_queries(1, W_LATE)
    back_rest(1, W_LATE, B_LATE)
    exchange(1)

    for copy in rn2_copies:
        copy.wait_recv()
    total = own[2, pl.ds(pl.multiple_of(zl * 64, 64), 64), :]
    for i in range(3):
        total = total + rn2[i].astype(F32)
    acc2[...] = total
    s2[...] = total.astype(BF)
    ry2_copies = []
    for i in range(3):
        rows = pl.multiple_of(lax.rem(y + i + 1, NY) * 16, 16)
        ry2_copies.append(
            send(s2.at[pl.ds(rows, 16), :], ry2.at[i], ry2s.at[i], ry2r.at[i], dev(dy=i + 1))
        )
    for copy in ry_copies:
        copy.wait_recv()
    for m in range(2):
        total = own[m, pl.ds(pl.multiple_of(y * 64, 64), 64), :]
        for i in range(3):
            total = total + ry[m, i].astype(F32)
        acc1[m] = total
        s1[m] = total.astype(BF)
    rn_copies = []
    for i, d in enumerate(near):
        rows = pl.multiple_of(lax.rem(z + d + NZ, 4) * 16, 16)
        rn_copies.append(
            send(s1.at[:, pl.ds(rows, 16), :], rn.at[i], rns.at[i], rnr.at[i], dev(dz=d))
        )

    x_relay(0)
    gather_end(W_EARLY)
    project(0)

    for copy in ry2_copies + rn_copies:
        copy.wait_recv()
    for m in range(2):
        total = acc1[m, pl.ds(pl.multiple_of(zl * 16, 16), 16), :]
        for i in range(3):
            total = total + rn[i, m].astype(F32)
        tile[m] = total
    total = acc2[pl.ds(pl.multiple_of(y * 16, 16), 16), :]
    for i in range(3):
        total = total + ry2[i].astype(F32)
    tile[2] = total
    for m in range(3):
        for k4 in range(4):
            piece = tile[m, pl.ds(4 * k4, 4), :]
            fsf[k4, m] = piece
            fs[k4, m] = piece.astype(BF)
    rf_copies = []
    for i, d in enumerate(fars):
        to = lax.rem(z + d + NZ, NZ) // 4
        rf_copies.append(send(fs.at[to], rf.at[i], rfs.at[i], rfr.at[i], dev(dz=d)))

    forward(0, W_EARLY)

    for copy in rf_copies:
        copy.wait_recv()
    total = adj[...] + fsf[zh]
    for i in range(3):
        total = total + rf[i].astype(F32)
    fb[B_EARLY, zh] = total.astype(BF)
    far_send(B_EARLY)

    back_queries(0, W_EARLY)
    heads_send(1)

    gather_far(B_EARLY)
    heads_end(1)
    gather_middle(B_EARLY)
    gather_end(B_EARLY)

    second(0, B_EARLY)
    back_rest(0, W_EARLY, B_EARLY)
    exchange(0)
    heads_send(0)
    heads_end(0)

    for copy in started:
        copy.wait_send()


def local(inputs, probe, address, payload, checkpoints, out_grad, adjoint, inner_rate):
    vmem = pl.BlockSpec(memory_space=pltpu.VMEM)
    dma = pltpu.SemaphoreType.DMA
    scratch = [
        pltpu.VMEM((2, T, D), BF),
        pltpu.VMEM((D, 3 * DH), BF),
        pltpu.VMEM((4, DH, 3 * DH), BF),
        pltpu.VMEM((4, 3, DH, F), BF),
        pltpu.VMEM((4, 4, 3, 4, F), BF),
        pltpu.VMEM((3, 16, F), F32),
        pltpu.VMEM((2, 3, T, DH), BF),
        pltpu.VMEM((2, T, DH), BF),
        pltpu.VMEM((2, 9, T, F), F32),
        pltpu.VMEM((2, 9, T, F), BF),
        pltpu.VMEM((3, DH, F), F32),
        pltpu.VMEM((3, DH, F), BF),
        pltpu.VMEM((2, 3, 64, F), BF),
        pltpu.VMEM((2, 64, F), F32),
        pltpu.VMEM((2, 64, F), BF),
        pltpu.VMEM((3, 2, 16, F), BF),
        pltpu.VMEM((3, 64, F), BF),
        pltpu.VMEM((64, F), F32),
        pltpu.VMEM((64, F), BF),
        pltpu.VMEM((3, 16, F), BF),
        pltpu.VMEM((4, 3, 4, F), BF),
        pltpu.VMEM((4, 3, 4, F), F32),
        pltpu.VMEM((3, 3, 4, F), BF),
        pltpu.VMEM((2, T, 3 * DH), BF),
        pltpu.VMEM((2, T, 3 * DH), BF),
        pltpu.VMEM((2, 3, T, DH), BF),
        pltpu.VMEM((2, 3, T, DH), BF),
    ]
    for shape in ((2, 7), (4, 3), (4, 3), (4, 3), (4, 3), (4, 3), (2, 3), (3,), (3,), (3,), (3,), (6,), (2, 3)):
        scratch += [dma(shape), dma(shape)]
    return pl.pallas_call(
        kernel,
        name="meta_gradient",
        out_shape=jax.ShapeDtypeStruct((2, T, DH), BF),
        in_specs=[vmem] * 7 + [pl.BlockSpec(memory_space=pltpu.SMEM)],
        out_specs=vmem,
        scratch_shapes=scratch,
        compiler_params=pltpu.CompilerParams(
            collective_id=0, has_side_effects=True, vmem_limit_bytes=60 * 2**20
        ),
    )(
        inputs,
        probe,
        address,
        payload,
        checkpoints.reshape(2, 3, 4, F),
        out_grad,
        adjoint.reshape(3, 4, F),
        inner_rate,
    )


def solution(mesh):
    split = Mesh(mesh.devices.reshape(NZ, NY, NX, NC), AXES)
    tok, head = ("z", "y"), ("x", "c")
    placed = (
        P(None, tok, head),
        P(None, head),
        P(None, head),
        P(None, head),
        P(None, None, head, tok, None),
        P(None, tok, head),
        P(None, head, tok, None),
        P(head),
    )
    return jax.shard_map(
        local, mesh=split, in_specs=placed, out_specs=P(None, tok, head), check_vma=False
    )
```

time: 376 us -> 102 us (0.27)
  waiting for transfers between devices: 130 us -> 0 us
  Pallas kernels: 0 us -> 99.4 us
  blocking collectives: 93.7 us -> 0 us
  starting transfers between devices: 65.8 us -> 0 us
  matrix products: 47.7 us -> 0 us
  local copies, waits for them, and re-layouts: 17.6 us -> 1.67 us
  between operations: 15.3 us -> 0.66 us
  other arithmetic: 4.34 us -> 0 us
    pallas_call x0 -> x1, Pallas kernels: none -> 99.4 us  [local(): pl.pallas_call(kernel, name='meta_gradient', out_shape=jax.ShapeDtypeStru...]
    all_gather x4 -> x0, blocking collectives: 93.7 us -> none  [gathered_by_axis(): nearer = lax.all_gather(value, axes[-1], axis=dim, tiled=True)]
    all_to_all x5 -> x0, starting transfers between devices: 65.6 us -> none  [the longest x3 37.8 us: copy_for_each(): return lax.all_to_all(copies, axis, split_axis=0, concat_axis=0, tiled=True)]
    unnamed x3 -> x0, waiting for transfers between devices: 63.3 us -> none
    all_to_all x5 -> x0, waiting for transfers between devices: 47.8 us -> none  [the longest x3 34.2 us: copy_for_each(): return lax.all_to_all(copies, axis, split_axis=0, concat_axis=0, tiled=True)]
    dot_general x39 -> x0, matrix products: 47.7 us -> none  [the longest x33 28.2 us: contracted_array(): return jnp.einsum(form, left, right, preferred_element_type=jnp.float32)]
    reduce_scatter x1 -> x0, waiting for transfers between devices: 19.2 us -> none  [sum_by_axis(): nearer = lax.psum_scatter(value, axes[0], scatter_dimension=dim, tiled=True)]
    reshape x3 -> x0, local copies, waits for them, and re-layouts: 4.85 us -> none  [the longest x2 4.58 us: cut_along(): value.reshape(*shape[:dim], size, shape[dim] // size, *shape[dim + 1:])]
  transfers between devices with their start and end apart: 7 -> 0, of which waited for: 5 -> 0; matrix products, arithmetic and copies ran while one was open for 17% -> 0% of each run, Pallas kernels for 0% -> 0%
where the time goes in v1:
time: 102 us
  Pallas kernels  99.4 us (97%)
  local copies, waits for them, and re-layouts  1.67 us (2%)
    pallas_call x1, Pallas kernels, local(): pl.pallas_call(kernel, name='meta_gradient', out_shape=jax.ShapeDtypeStru...  99.4 us

profile of v1, /device:TPU:1, one launch (start us, length us, event | category | flops | bytes accessed | tf_op | source)
XLA Modules:
  0.0 101.7 jit_solution(15127845654504187788)
XLA Ops:
  0.7 99.4 %meta_gradient.1 = bf16[2,256,256]{2,1,0:T(8,128)(2,1)} custom-call(bf16[2,256,256]{2,1,0:T(8,128)(2,1)} %xin.1, bf16[2048,256]{1,0:T(8,128)(2,1)} %pq.1, bf16[2048,256]{1,0:T(8,128)(2,1)} %pk.1, bf16[2048,256]{1,0:T(8,128)(2,1)} %pv.1, bf16[2,3,4,512]{3,2,1,0:T(4,128)(2,1)} %bitcast.2, bf16[2,256,256]{2,1,0:T(8,128)(2,1)} %og.1, f32[3,4,512]{2,1,0:T(4,128)} %bitcast.3, ...), custom_call_target="tpu_custom_call" | custom-call | tf_op jit(solution)/shard_map/meta_gradient/pallas_call | solution.py:429
  100.1 1.7 %copy.11 = bf16[2,256,256]{2,1,0:T(8,128)(2,1)} copy(bf16[2,256,256]{2,1,0:T(8,128)(2,1)} %meta_gradient.1) | data formatting | bytes 524288

commit v2 on v1

v2 whole, which is shorter than its diff:
```python
import jax
import jax.numpy as jnp
from jax import lax
from jax.experimental import pallas as pl
from jax.experimental.pallas import tpu as pltpu
from jax.sharding import Mesh
from jax.sharding import PartitionSpec as P

AXES = ("z", "y", "x", "c")
NZ, NY, NX, NC = 16, 4, 4, 2
MESH = pl.DeviceIdType.MESH
BF = jnp.bfloat16
F32 = jnp.float32
T = 256
DH = 256
F = 512
D = 2048
W_LATE, B_LATE, W_EARLY, B_EARLY = 0, 1, 2, 3


def mm(a, b):
    return jnp.dot(a, b, preferred_element_type=F32)


def mm_t(a, b):
    return lax.dot_general(a, b, (((1,), (1,)), ((), ())), preferred_element_type=F32)


def t_mm(a, b):
    return lax.dot_general(a, b, (((0,), (0,)), ((), ())), preferred_element_type=F32)


def permutation():
    row = lax.broadcasted_iota(jnp.int32, (DH, DH), 0)
    place = lax.broadcasted_iota(jnp.int32, (DH, DH), 1)
    held = 64 * ((place // 4) % 4) + 16 * ((place // 16) % 4) + 4 * (place // 64) + place % 4
    return jnp.where(row == held, 1.0, 0.0).astype(BF)


def kernel(
    xin, pq, pk, pv, ck, og, adj, rate, out,
    xg, pr, pc, pp, gath, fb, adjv, tile, ogv, qkv, o_s, fw, hb, own, rsend,
    r1, acc, sd, r2, part, fsend, rf, gcat, gp, pb, ro,
    ls, xs, xr, fs, fr, as_, ar, bs, br, r1s, r1r, r2s, r2r, rfs, rfr, cs, cr, hs, hr,
):
    z, y = lax.axis_index("z"), lax.axis_index("y")
    x, c = lax.axis_index("x"), lax.axis_index("c")

    def dev(dz=0, dy=0, dx=0, dc=0):
        return (
            lax.rem(z + dz + NZ, NZ), lax.rem(y + dy, NY), lax.rem(x + dx, NX), lax.rem(c + dc, NC)
        )

    zh, zl = z // 4, lax.rem(z, 4)
    skip = 4 * c - 2
    near = [1, -1, skip]

    barrier = pltpu.get_barrier_semaphore()
    partners = [dev(dz=d) for d in (4, -4, 2, -2, 1, -1)]
    partners += [dev(dy=d) for d in (1, 2, 3)] + [dev(dx=d) for d in (1, 2, 3)] + [dev(dc=1)]
    for partner in partners:
        pl.semaphore_signal(barrier, inc=1, device_id=partner, device_id_type=MESH)

    started = []

    def send(src, dst, ssem, rsem, device):
        copy = pltpu.make_async_remote_copy(
            src_ref=src, dst_ref=dst, send_sem=ssem, recv_sem=rsem,
            device_id=device, device_id_type=MESH,
        )
        copy.start()
        started.append(copy)
        return copy

    column = pl.multiple_of((x * 2 + c) * DH, DH)
    loads = [
        pltpu.make_async_copy(src, dst, ls.at[i])
        for i, (src, dst) in enumerate((
            (ck.at[1], fb.at[W_LATE, zh]),
            (adj, adjv),
            (ck.at[0], fb.at[W_EARLY, zh]),
            (xin.at[1], xg.at[1, :, pl.ds(column, DH)]),
            (pq, pr.at[0]),
            (pk, pr.at[1]),
            (pv, pr.at[2]),
            (og, ogv),
            (xin.at[0], xg.at[0, :, pl.ds(column, DH)]),
        ))
    ]
    for load in loads:
        load.start()
    for load in loads[:4]:
        load.wait()
    fb[B_LATE, zh] = adjv[...].astype(BF)

    pl.semaphore_wait(barrier, len(partners))

    far_copies = {}

    def far_send(i, sets):
        piece = fb.at[sets, zh]
        far_copies[i] = [
            send(piece, piece, fs.at[i, n], fr.at[i, n], dev(dz=d)) for n, d in enumerate((4, -4))
        ]

    def far_relay(i, sets):
        for copy in far_copies[i]:
            copy.wait_recv()
        below = fb.at[sets, lax.rem(zh + 3, 4), pl.ds(0, 1)]
        above = fb.at[sets, lax.rem(zh + 1, 4), pl.ds(1, 2)]
        far_copies[i] = [
            send(below, below, fs.at[i, 2], fr.at[i, 2], dev(dz=4)),
            send(above, above, fs.at[i, 3], fr.at[i, 3], dev(dz=-4)),
        ]

    x_copies = {}

    def x_send(s):
        block = xg.at[s, :, pl.ds(column, DH)]
        x_copies[s] = [
            send(xin.at[s], block, xs.at[s, i], xr.at[s, i], dev(dx=d)) for i, d in enumerate((2, 1, 3))
        ]
        x_copies[s].append(send(xin.at[s], block, xs.at[s, 3], xr.at[s, 3], dev(dc=1)))

    late, early = pl.ds(0, 2), pl.ds(2, 1)
    far_send(0, late)
    x_send(1)
    far_send(1, early)
    x_send(0)

    order = permutation()
    for i in range(3):
        loads[4 + i].wait()
        for j in range(8):
            rows = pl.ds(j * DH, DH)
            pc[rows, pl.ds(i * DH, DH)] = mm(pr[i, rows, :], order).astype(BF)

    far_relay(0, late)
    far_relay(1, early)

    other = 1 - c
    pc_copies = []
    for i in range(4):
        rows = pl.multiple_of((i * 2 + other) * DH, DH)
        pc_copies.append(
            send(pc.at[pl.ds(rows, DH), :], pp.at[i], cs.at[i], cr.at[i], dev(dc=1))
        )
    loads[7].wait()
    for s in range(2):
        o_s[s] = mm(ogv[s], order).astype(BF)

    first, last = {}, {}

    def to_near(block, ssem, rsem):
        return [send(block, block, ssem.at[i], rsem.at[i], dev(dz=d)) for i, d in enumerate(near)]

    def to_y(block, ssem, rsem):
        return [send(block, block, ssem.at[i], rsem.at[i], dev(dy=d)) for i, d in enumerate((2, 1, 3))]

    def swapped(s, half):
        return half == 1 and s != W_EARLY

    def gather_first(s):
        first[s] = []
        for half in range(2):
            block = gath.at[s, half, :, y, zl]
            stage = to_y if swapped(s, half) else to_near
            first[s] += stage(block, as_.at[s, half], ar.at[s, half])

    def gather_last(s):
        for copy in first[s]:
            copy.wait_recv()
        last[s] = []
        for half in range(2):
            if swapped(s, half):
                last[s] += to_near(gath.at[s, half, :, :, zl], bs.at[s, half], br.at[s, half])
            else:
                last[s] += to_y(gath.at[s, half, :, y], bs.at[s, half], br.at[s, half])

    def gather_end(s):
        for copy in last[s]:
            copy.wait_recv()

    def far_end(i):
        for copy in far_copies[i]:
            copy.wait_recv()

    def assemble(s):
        for m in range(3):
            for k in range(4):
                tile[m, pl.ds(4 * k, 4), :] = fb[s, k, m].astype(F32)
            gath[s, 0, m, y, zl] = tile[m, :, pl.ds(0, 256)].astype(BF)
            gath[s, 1, m, y, zl] = tile[m, :, pl.ds(256, 256)].astype(BF)

    relays = {}

    def x_relay(s):
        relays[s] = []
        for i, d in enumerate((2, 1, 3)):
            x_copies[s][i].wait_recv()
            source = pl.multiple_of((lax.rem(x + 4 - d, NX) * 2 + c) * DH, DH)
            block = xg.at[s, :, pl.ds(source, DH)]
            relays[s].append(send(block, block, xs.at[s, 4 + i], xr.at[s, 4 + i], dev(dc=1)))

    def project(s):
        for copy in [x_copies[s][3]] + relays[s]:
            copy.wait_recv()
        for i in range(3):
            qkv[s, i] = mm(xg[s], pc[:, pl.ds(i * DH, DH)]).astype(BF)

    factor = rate[0] / 16384.0

    def weight(s, half, m):
        return gath[s, half, m].reshape(DH, 256)

    def ahead(rows, s, m, to):
        for half in range(2):
            fw[to[0], to[1], :, pl.ds(half * 256, 256)] = mm(rows, weight(s, half, m))

    def behind(s, i, w, m):
        return mm_t(hb[s, i, :, pl.ds(0, 256)], weight(w, 0, m)) + mm_t(
            hb[s, i, :, pl.ds(256, 256)], weight(w, 1, m)
        )

    def forward(s, w):
        q, k, v = qkv[s, 0], qkv[s, 1], qkv[s, 2]
        ahead(q, w, 0, (s, 0))
        ahead(q, w, 1, (s, 1))
        ahead(o_s[s], w, 2, (s, 2))
        ahead(k, w, 0, (s, 3))
        ahead(k, w, 1, (s, 4))
        ahead(v, w, 2, (s, 5))

        @pl.loop(0, T // 16)
        def _(step):
            rows = pl.ds(pl.multiple_of(step * 16, 16), 16)
            gate, lift, back = fw[s, 0, rows, :], fw[s, 1, rows, :], fw[s, 2, rows, :]
            g = jax.nn.sigmoid(gate)
            act = gate * g
            if s > 0:
                hb[s, 0, rows, :] = (act * lift).astype(BF)
            hb[s, 1, rows, :] = (back * lift * (g * (1.0 + gate * (1.0 - g)))).astype(BF)
            hb[s, 2, rows, :] = (back * act).astype(BF)
            gate, u, e = fw[s, 3, rows, :], fw[s, 4, rows, :], fw[s, 5, rows, :]
            g = jax.nn.sigmoid(gate)
            act = factor * gate * g
            slope = factor * (g * (1.0 + gate * (1.0 - g)))
            bend = factor * (g * (1.0 - g) * (2.0 + gate * (1.0 - 2.0 * g)))
            us = u * slope
            fw[s, 0, rows, :] = us
            fw[s, 1, rows, :] = e * u * bend
            fw[s, 2, rows, :] = e * slope
            fw[s, 3, rows, :] = act
            hb[s, 6, rows, :] = (act * u).astype(BF)
            hb[s, 7, rows, :] = (e * us).astype(BF)
            hb[s, 8, rows, :] = (e * act).astype(BF)

    def second(s, b):
        ahead(qkv[s, 2], b, 2, (s, 6))
        ahead(qkv[s, 1], b, 0, (s, 7))
        ahead(qkv[s, 1], b, 1, (s, 8))

        @pl.loop(0, T // 16)
        def _(step):
            rows = pl.ds(pl.multiple_of(step * 16, 16), 16)
            pull, one, three = fw[s, 6, rows, :], fw[s, 7, rows, :], fw[s, 8, rows, :]
            us, eub, es, act = (fw[s, i, rows, :] for i in range(4))
            hb[s, 3, rows, :] = (us * pull + one * eub + three * es).astype(BF)
            hb[s, 4, rows, :] = (act * pull + one * es).astype(BF)
            hb[s, 5, rows, :] = (one * us + three * act).astype(BF)

    def back_queries(s, w):
        grad = behind(s, 1, w, 0) + behind(s, 2, w, 1)
        gcat[s, :, pl.ds(0, DH)] = grad.astype(BF)

    def back_rest(s, w, b):
        grad = behind(s, 3, w, 0) + behind(s, 4, w, 1)
        grad = grad + behind(s, 7, b, 0) + behind(s, 8, b, 1)
        gcat[s, :, pl.ds(DH, DH)] = grad.astype(BF)
        grad = behind(s, 5, w, 2) + behind(s, 6, b, 2)
        gcat[s, :, pl.ds(2 * DH, DH)] = grad.astype(BF)

    pair = {}

    def exchange(s):
        pair[s] = send(gcat.at[s], gp.at[s], cs.at[4 + s], cr.at[4 + s], dev(dc=1))

    heads = {}

    def partial_of(s, step):
        to = lax.rem(x + step, NX)
        rows = pl.multiple_of((to * 2 + c) * DH, DH)
        return mm_t(gcat[s], pc[pl.ds(rows, DH), :]) + mm_t(gp[s], pp[to])

    def heads_send(s):
        if s == 1:
            for copy in pc_copies:
                copy.wait_recv()
        pair[s].wait_recv()
        heads[s] = []
        for i, step in enumerate((2, 1, 3)):
            pb[s, i] = partial_of(s, step).astype(BF)
            heads[s].append(
                send(pb.at[s, i], ro.at[s, i], hs.at[s, i], hr.at[s, i], dev(dx=step))
            )

    def heads_end(s):
        total = partial_of(s, 0)
        for i in range(3):
            heads[s][i].wait_recv()
            total = total + ro[s, i].astype(F32)
        out[s] = total.astype(BF)

    far_end(0)
    assemble(W_LATE)
    gather_first(W_LATE)
    assemble(B_LATE)
    gather_first(B_LATE)
    gather_last(W_LATE)
    gather_last(B_LATE)
    x_relay(1)
    far_end(1)
    assemble(W_EARLY)
    gather_first(W_EARLY)
    project(1)
    gather_end(W_LATE)
    forward(1, W_LATE)
    gather_end(B_LATE)
    second(1, B_LATE)

    terms = (
        (qkv[1, 1], 3, qkv[1, 0], 1),
        (qkv[1, 1], 4, qkv[1, 0], 2),
        (qkv[1, 2], 5, o_s[1], 0),
    )
    sum_a, sum_b = {}, {}
    for m, (left, i, right, j) in enumerate(terms):
        for half in range(2):
            lanes = pl.ds(half * 256, 256)
            grad = t_mm(left, hb[1, i, :, lanes]) + t_mm(right, hb[1, j, :, lanes])
            grad = grad.reshape(4, 4, 16, 256)
            own[half, m] = grad
            rsend[half, m] = grad.astype(BF)
        sum_a[m] = [
            send(rsend.at[0, m, lax.rem(y + d, NY)], r1.at[0, m, n],
                 r1s.at[0, m, n], r1r.at[0, m, n], dev(dy=d))
            for n, d in enumerate((2, 1, 3))
        ]
        sum_b[m] = [
            send(rsend.at[1, m, :, lax.rem(z + d + NZ, 4)], r1.at[1, m, n],
                 r1s.at[1, m, n], r1r.at[1, m, n], dev(dz=d))
            for n, d in enumerate(near)
        ]

    back_queries(1, W_LATE)
    back_rest(1, W_LATE, B_LATE)
    exchange(1)

    for m in range(3):
        for copy in sum_a[m]:
            copy.wait_recv()
        total = own[0, m, y]
        for i in range(3):
            total = total + r1[0, m, i].astype(F32)
        acc[0, m] = total
        sd[0, m] = total.astype(BF)
        for copy in sum_b[m]:
            copy.wait_recv()
        total = own[1, m, :, zl]
        for i in range(3):
            total = total + r1[1, m, i].astype(F32)
        acc[1, m] = total
        sd[1, m] = total.astype(BF)
    two_a = [
        send(sd.at[0, :, lax.rem(z + d + NZ, 4)], r2.at[0, n], r2s.at[0, n], r2r.at[0, n], dev(dz=d))
        for n, d in enumerate(near)
    ]
    two_b = [
        send(sd.at[1, :, lax.rem(y + d, NY)], r2.at[1, n], r2s.at[1, n], r2r.at[1, n], dev(dy=d))
        for n, d in enumerate((2, 1, 3))
    ]

    x_relay(0)
    loads[8].wait()
    project(0)

    flip = 4 - 8 * lax.rem(zh, 2)
    third = {}

    def far_sum(half, step):
        fsend[half, step] = part[half].astype(BF)
        way = flip if half == step else -flip
        third[half] = send(
            fsend.at[half, step], rf.at[half, step], rfs.at[half, step], rfr.at[half, step], dev(dz=way)
        )

    for half, copies, place in ((0, two_a, zl), (1, two_b, y)):
        for copy in copies:
            copy.wait_recv()
        total = acc[half, :, place]
        for i in range(3):
            total = total + r2[half, i].astype(F32)
        part[half] = total
        for k in range(4):
            mine = jnp.where(zh == k, 1.0, 0.0)
            for m in range(3):
                rows = pl.ds(4 * k, 4)
                part[half, m, rows, :] = (
                    part[half, m, rows, :] + mine * adjv[m, :, pl.ds(half * 256, 256)]
                )
        far_sum(half, 0)

    gather_last(W_EARLY)
    for half in range(2):
        third[half].wait_recv()
        part[half] = part[half] + rf[half, 0].astype(F32)
        far_sum(half, 1)
    heads_send(1)
    for half in range(2):
        third[half].wait_recv()
        gath[B_EARLY, half, :, y, zl] = (part[half] + rf[half, 1].astype(F32)).astype(BF)
    gather_first(B_EARLY)
    gather_end(W_EARLY)
    gather_last(B_EARLY)
    forward(0, W_EARLY)
    back_queries(0, W_EARLY)
    heads_end(1)
    gather_end(B_EARLY)

    second(0, B_EARLY)
    back_rest(0, W_EARLY, B_EARLY)
    exchange(0)
    heads_send(0)
    heads_end(0)

    for copy in started:
        copy.wait_send()


def local(inputs, probe, address, payload, checkpoints, out_grad, adjoint, inner_rate):
    hbm = pl.BlockSpec(memory_space=pl.ANY)
    dma = pltpu.SemaphoreType.DMA
    scratch = [
        pltpu.VMEM((2, T, D), BF),
        pltpu.VMEM((3, D, DH), BF),
        pltpu.VMEM((D, 3 * DH), BF),
        pltpu.VMEM((4, DH, 3 * DH), BF),
        pltpu.VMEM((4, 2, 3, 4, 4, 16, 256), BF),
        pltpu.VMEM((3, 4, 3, 4, F), BF),
        pltpu.VMEM((3, 4, F), F32),
        pltpu.VMEM((3, 16, F), F32),
        pltpu.VMEM((2, T, DH), BF),
        pltpu.VMEM((2, 3, T, DH), BF),
        pltpu.VMEM((2, T, DH), BF),
        pltpu.VMEM((2, 9, T, F), F32),
        pltpu.VMEM((2, 9, T, F), BF),
        pltpu.VMEM((2, 3, 4, 4, 16, 256), F32),
        pltpu.VMEM((2, 3, 4, 4, 16, 256), BF),
        pltpu.VMEM((2, 3, 3, 4, 16, 256), BF),
        pltpu.VMEM((2, 3, 4, 16, 256), F32),
        pltpu.VMEM((2, 3, 4, 16, 256), BF),
        pltpu.VMEM((2, 3, 3, 16, 256), BF),
        pltpu.VMEM((2, 3, 16, 256), F32),
        pltpu.VMEM((2, 2, 3, 16, 256), BF),
        pltpu.VMEM((2, 2, 3, 16, 256), BF),
        pltpu.VMEM((2, T, 3 * DH), BF),
        pltpu.VMEM((2, T, 3 * DH), BF),
        pltpu.VMEM((2, 3, T, DH), BF),
        pltpu.VMEM((2, 3, T, DH), BF),
        dma((9,)),
    ]
    for shape in ((2, 7), (2, 4), (4, 2, 3), (4, 2, 3), (2, 3, 3), (2, 3), (2, 2), (6,), (2, 3)):
        scratch += [dma(shape), dma(shape)]
    return pl.pallas_call(
        kernel,
        name="meta_gradient",
        out_shape=jax.ShapeDtypeStruct((2, T, DH), BF),
        in_specs=[hbm] * 7 + [pl.BlockSpec(memory_space=pltpu.SMEM)],
        out_specs=pl.BlockSpec(memory_space=pltpu.VMEM),
        scratch_shapes=scratch,
        compiler_params=pltpu.CompilerParams(
            collective_id=0, has_side_effects=True, vmem_limit_bytes=60 * 2**20
        ),
    )(
        inputs,
        probe,
        address,
        payload,
        checkpoints.reshape(2, 3, 4, F),
        out_grad,
        adjoint.reshape(3, 4, F),
        inner_rate,
    )


def solution(mesh):
    split = Mesh(mesh.devices.reshape(NZ, NY, NX, NC), AXES)
    tok, head = ("z", "y"), ("x", "c")
    placed = (
        P(None, tok, head),
        P(None, head),
        P(None, head),
        P(None, head),
        P(None, None, head, tok, None),
        P(None, tok, head),
        P(None, head, tok, None),
        P(head),
    )
    return jax.shard_map(
        local, mesh=split, in_specs=placed, out_specs=P(None, tok, head), check_vma=False
    )
```

time: 102 us -> 88.7 us (0.87)
  Pallas kernels: 99.4 us -> 86.2 us
    pallas_call x1, Pallas kernels: 99.4 us -> 86.2 us  [local(): pl.pallas_call(kernel, name='meta_gradient', out_shape=jax.ShapeDtypeStru...]
where the time goes in v2:
time: 88.7 us; the launch traced here: 88.6 us
  Pallas kernels  86.2 us (97%)
  local copies, waits for them, and re-layouts  1.67 us (2%)
    pallas_call x1, Pallas kernels, local(): pl.pallas_call(kernel, name='meta_gradient', out_shape=jax.ShapeDtypeStru...  86.2 us

profile of v2, /device:TPU:1, one launch (start us, length us, event | category | flops | bytes accessed | tf_op | source)
XLA Modules:
  0.0 88.6 jit_solution(917120084552723415)
XLA Ops:
  0.7 86.2 %meta_gradient.1 = bf16[2,256,256]{2,1,0:T(8,128)(2,1)} custom-call(bf16[2,256,256]{2,1,0:T(8,128)(2,1)} %xin.1, bf16[2048,256]{1,0:T(8,128)(2,1)} %pq.1, bf16[2048,256]{1,0:T(8,128)(2,1)} %pk.1, bf16[2048,256]{1,0:T(8,128)(2,1)} %pv.1, bf16[2,3,4,512]{3,2,1,0:T(4,128)(2,1)} %bitcast.2, bf16[2,256,256]{2,1,0:T(8,128)(2,1)} %og.1, f32[3,4,512]{2,1,0:T(4,128)} %bitcast.3, ...), custom_call_target="tpu_custom_call" | custom-call | tf_op jit(solution)/shard_map/meta_gradient/pallas_call | solution.py:474
  86.9 1.7 %copy.11 = bf16[2,256,256]{2,1,0:T(8,128)(2,1)} copy(bf16[2,256,256]{2,1,0:T(8,128)(2,1)} %meta_gradient.1) | data formatting | bytes 524288

commit v3 on v2

--- a/solution.py
+++ b/solution.py
@@ -40,8 +40,8 @@
 def kernel(
     xin, pq, pk, pv, ck, og, adj, rate, out,
     xg, pr, pc, pp, gath, fb, adjv, tile, ogv, qkv, o_s, fw, hb, own, rsend,
-    r1, acc, sd, r2, part, fsend, rf, gcat, gp, pb, ro,
-    ls, xs, xr, fs, fr, as_, ar, bs, br, r1s, r1r, r2s, r2r, rfs, rfr, cs, cr, hs, hr,
+    r1, acc, sd, r2, part, fsend, rf, gcat, gp, back, base, pb, ro,
+    ls, xs, xr, fs, fr, as_, ar, bs, br, r1s, r1r, r2s, r2r, rfs, rfr, cs, cr, ps, pr_, hs, hr,
 ):
     z, y = lax.axis_index("z"), lax.axis_index("y")
     x, c = lax.axis_index("x"), lax.axis_index("c")
@@ -97,17 +97,17 @@
 
     far_copies = {}
 
-    def far_send(i, sets):
-        piece = fb.at[sets, zh]
+    def far_send(i):
+        piece = fb.at[i, zh]
         far_copies[i] = [
             send(piece, piece, fs.at[i, n], fr.at[i, n], dev(dz=d)) for n, d in enumerate((4, -4))
         ]
 
-    def far_relay(i, sets):
+    def far_relay(i):
         for copy in far_copies[i]:
             copy.wait_recv()
-        below = fb.at[sets, lax.rem(zh + 3, 4), pl.ds(0, 1)]
-        above = fb.at[sets, lax.rem(zh + 1, 4), pl.ds(1, 2)]
+        below = fb.at[i, lax.rem(zh + 3, 4), pl.ds(0, 1)]
+        above = fb.at[i, lax.rem(zh + 1, 4), pl.ds(1, 2)]
         far_copies[i] = [
             send(below, below, fs.at[i, 2], fr.at[i, 2], dev(dz=4)),
             send(above, above, fs.at[i, 3], fr.at[i, 3], dev(dz=-4)),
@@ -122,10 +122,10 @@
         ]
         x_copies[s].append(send(xin.at[s], block, xs.at[s, 3], xr.at[s, 3], dev(dc=1)))
 
-    late, early = pl.ds(0, 2), pl.ds(2, 1)
-    far_send(0, late)
+    far_send(W_LATE)
+    far_send(B_LATE)
     x_send(1)
-    far_send(1, early)
+    far_send(W_EARLY)
     x_send(0)
 
     order = permutation()
@@ -135,8 +135,9 @@
             rows = pl.ds(j * DH, DH)
             pc[rows, pl.ds(i * DH, DH)] = mm(pr[i, rows, :], order).astype(BF)
 
-    far_relay(0, late)
-    far_relay(1, early)
+    far_relay(W_LATE)
+    far_relay(B_LATE)
+    far_relay(W_EARLY)
 
     other = 1 - c
     pc_copies = []
@@ -157,25 +158,21 @@
     def to_y(block, ssem, rsem):
         return [send(block, block, ssem.at[i], rsem.at[i], dev(dy=d)) for i, d in enumerate((2, 1, 3))]
 
-    def swapped(s, half):
-        return half == 1 and s != W_EARLY
-
-    def gather_first(s):
-        first[s] = []
-        for half in range(2):
-            block = gath.at[s, half, :, y, zl]
-            stage = to_y if swapped(s, half) else to_near
-            first[s] += stage(block, as_.at[s, half], ar.at[s, half])
-
-    def gather_last(s):
-        for copy in first[s]:
-            copy.wait_recv()
-        last[s] = []
-        for half in range(2):
-            if swapped(s, half):
-                last[s] += to_near(gath.at[s, half, :, :, zl], bs.at[s, half], br.at[s, half])
-            else:
-                last[s] += to_y(gath.at[s, half, :, y], bs.at[s, half], br.at[s, half])
+    def gather_first(s, m=None):
+        index = s if m is None else s + m
+        mats = pl.ds(0, 3) if m is None else m
+        first[index] = []
+        for half, stage in ((0, to_near), (1, to_y)):
+            block = gath.at[s, half, mats, y, zl]
+            first[index] += stage(block, as_.at[index, half], ar.at[index, half])
+
+    def gather_last(s, m=None):
+        index = s if m is None else s + m
+        mats = pl.ds(0, 3) if m is None else m
+        for copy in first[index]:
+            copy.wait_recv()
+        last[index] = to_y(gath.at[s, 0, mats, y], bs.at[index, 0], br.at[index, 0])
+        last[index] += to_near(gath.at[s, 1, mats, :, zl], bs.at[index, 1], br.at[index, 1])
 
     def gather_end(s):
         for copy in last[s]:
@@ -255,11 +252,10 @@
             hb[s, 7, rows, :] = (e * us).astype(BF)
             hb[s, 8, rows, :] = (e * act).astype(BF)
 
-    def second(s, b):
-        ahead(qkv[s, 2], b, 2, (s, 6))
-        ahead(qkv[s, 1], b, 0, (s, 7))
-        ahead(qkv[s, 1], b, 1, (s, 8))
-
+    def sides(s, b, m):
+        ahead(qkv[s, 1] if m < 2 else qkv[s, 2], b, m, (s, (7, 8, 6)[m]))
+
+    def second(s):
         @pl.loop(0, T // 16)
         def _(step):
             rows = pl.ds(pl.multiple_of(step * 16, 16), 16)
@@ -273,60 +269,77 @@
         grad = behind(s, 1, w, 0) + behind(s, 2, w, 1)
         gcat[s, :, pl.ds(0, DH)] = grad.astype(BF)
 
-    def back_rest(s, w, b):
-        grad = behind(s, 3, w, 0) + behind(s, 4, w, 1)
-        grad = grad + behind(s, 7, b, 0) + behind(s, 8, b, 1)
+    def back_sides(s, b):
+        back[0] = behind(s, 7, b, 0) + behind(s, 8, b, 1)
+        back[1] = behind(s, 6, b, 2)
+
+    def back_rest(s, w):
+        grad = behind(s, 3, w, 0) + behind(s, 4, w, 1) + back[0]
         gcat[s, :, pl.ds(DH, DH)] = grad.astype(BF)
-        grad = behind(s, 5, w, 2) + behind(s, 6, b, 2)
+        grad = behind(s, 5, w, 2) + back[1]
         gcat[s, :, pl.ds(2 * DH, DH)] = grad.astype(BF)
 
     pair = {}
-
-    def exchange(s):
-        pair[s] = send(gcat.at[s], gp.at[s], cs.at[4 + s], cr.at[4 + s], dev(dc=1))
+    query_part, rest_part = pl.ds(0, DH), pl.ds(DH, 2 * DH)
+
+    def exchange(s, i, lanes):
+        pair[s, i] = send(
+            gcat.at[s, :, lanes], gp.at[s, :, lanes], ps.at[s, i], pr_.at[s, i], dev(dc=1)
+        )
 
     heads = {}
-
-    def partial_of(s, step):
-        to = lax.rem(x + step, NX)
-        rows = pl.multiple_of((to * 2 + c) * DH, DH)
-        return mm_t(gcat[s], pc[pl.ds(rows, DH), :]) + mm_t(gp[s], pp[to])
+    steps = (2, 1, 3, 0)
+
+    def own_term(s, step, lanes):
+        rows = pl.multiple_of((lax.rem(x + step, NX) * 2 + c) * DH, DH)
+        return mm_t(gcat[s, :, lanes], pc[pl.ds(rows, DH), lanes])
+
+    def pair_term(s, step, lanes):
+        return mm_t(gp[s, :, lanes], pp[lax.rem(x + step, NX), :, lanes])
+
+    def heads_queries(s):
+        pair[s, 0].wait_recv()
+        for i, step in enumerate(steps):
+            base[i] = own_term(s, step, query_part) + pair_term(s, step, query_part)
 
     def heads_send(s):
-        if s == 1:
-            for copy in pc_copies:
-                copy.wait_recv()
-        pair[s].wait_recv()
+        for i, step in enumerate(steps):
+            base[i] = base[i] + own_term(s, step, rest_part)
+        pair[s, 1].wait_recv()
         heads[s] = []
-        for i, step in enumerate((2, 1, 3)):
-            pb[s, i] = partial_of(s, step).astype(BF)
+        for i, step in enumerate(steps[:3]):
+            pb[s, i] = (base[i] + pair_term(s, step, rest_part)).astype(BF)
             heads[s].append(
                 send(pb.at[s, i], ro.at[s, i], hs.at[s, i], hr.at[s, i], dev(dx=step))
             )
+        base[3] = base[3] + pair_term(s, 0, rest_part)
 
     def heads_end(s):
-        total = partial_of(s, 0)
+        total = base[3]
         for i in range(3):
             heads[s][i].wait_recv()
             total = total + ro[s, i].astype(F32)
         out[s] = total.astype(BF)
 
-    far_end(0)
-    assemble(W_LATE)
-    gather_first(W_LATE)
-    assemble(B_LATE)
-    gather_first(B_LATE)
+    x_relay(1)
+    for s in (W_LATE, B_LATE, W_EARLY):
+        far_end(s)
+        assemble(s)
+        gather_first(s)
+    project(1)
     gather_last(W_LATE)
     gather_last(B_LATE)
-    x_relay(1)
-    far_end(1)
-    assemble(W_EARLY)
-    gather_first(W_EARLY)
-    project(1)
+    x_relay(0)
+    loads[8].wait()
+    project(0)
     gather_end(W_LATE)
+    gather_last(W_EARLY)
     forward(1, W_LATE)
+    back_queries(1, W_LATE)
     gather_end(B_LATE)
-    second(1, B_LATE)
+    for m in range(3):
+        sides(1, B_LATE, m)
+    second(1)
 
     terms = (
         (qkv[1, 1], 3, qkv[1, 0], 1),
@@ -352,10 +365,12 @@
             for n, d in enumerate(near)
         ]
 
-    back_queries(1, W_LATE)
-    back_rest(1, W_LATE, B_LATE)
-    exchange(1)
-
+    exchange(1, 0, query_part)
+    back_sides(1, B_LATE)
+    back_rest(1, W_LATE)
+    exchange(1, 1, rest_part)
+
+    two = {}
     for m in range(3):
         for copy in sum_a[m]:
             copy.wait_recv()
@@ -364,6 +379,11 @@
             total = total + r1[0, m, i].astype(F32)
         acc[0, m] = total
         sd[0, m] = total.astype(BF)
+        two[0, m] = [
+            send(sd.at[0, m, lax.rem(z + d + NZ, 4)], r2.at[0, m, n],
+                 r2s.at[0, m, n], r2r.at[0, m, n], dev(dz=d))
+            for n, d in enumerate(near)
+        ]
         for copy in sum_b[m]:
             copy.wait_recv()
         total = own[1, m, :, zl]
@@ -371,65 +391,73 @@
             total = total + r1[1, m, i].astype(F32)
         acc[1, m] = total
         sd[1, m] = total.astype(BF)
-    two_a = [
-        send(sd.at[0, :, lax.rem(z + d + NZ, 4)], r2.at[0, n], r2s.at[0, n], r2r.at[0, n], dev(dz=d))
-        for n, d in enumerate(near)
-    ]
-    two_b = [
-        send(sd.at[1, :, lax.rem(y + d, NY)], r2.at[1, n], r2s.at[1, n], r2r.at[1, n], dev(dy=d))
-        for n, d in enumerate((2, 1, 3))
-    ]
-
-    x_relay(0)
-    loads[8].wait()
-    project(0)
+        two[1, m] = [
+            send(sd.at[1, m, lax.rem(y + d, NY)], r2.at[1, m, n],
+                 r2s.at[1, m, n], r2r.at[1, m, n], dev(dy=d))
+            for n, d in enumerate((2, 1, 3))
+        ]
 
     flip = 4 - 8 * lax.rem(zh, 2)
     third = {}
 
-    def far_sum(half, step):
-        fsend[half, step] = part[half].astype(BF)
+    def far_sum(half, m, step):
+        fsend[half, step, m] = part[half, m].astype(BF)
         way = flip if half == step else -flip
-        third[half] = send(
-            fsend.at[half, step], rf.at[half, step], rfs.at[half, step], rfr.at[half, step], dev(dz=way)
+        third[half, m] = send(
+            fsend.at[half, step, m], rf.at[half, step, m],
+            rfs.at[half, step, m], rfr.at[half, step, m], dev(dz=way)
         )
 
-    for half, copies, place in ((0, two_a, zl), (1, two_b, y)):
-        for copy in copies:
-            copy.wait_recv()
-        total = acc[half, :, place]
-        for i in range(3):
-            total = total + r2[half, i].astype(F32)
-        part[half] = total
-        for k in range(4):
-            mine = jnp.where(zh == k, 1.0, 0.0)
-            for m in range(3):
+    for m in range(3):
+        for half, place in ((0, zl), (1, y)):
+            for copy in two[half, m]:
+                copy.wait_recv()
+            total = acc[half, m, place]
+            for i in range(3):
+                total = total + r2[half, m, i].astype(F32)
+            part[half, m] = total
+            for k in range(4):
+                mine = jnp.where(zh == k, 1.0, 0.0)
                 rows = pl.ds(4 * k, 4)
                 part[half, m, rows, :] = (
                     part[half, m, rows, :] + mine * adjv[m, :, pl.ds(half * 256, 256)]
                 )
-        far_sum(half, 0)
-
-    gather_last(W_EARLY)
-    for half in range(2):
-        third[half].wait_recv()
-        part[half] = part[half] + rf[half, 0].astype(F32)
-        far_sum(half, 1)
+            far_sum(half, m, 0)
+
+    gather_end(W_EARLY)
+    forward(0, W_EARLY)
+
+    for m in range(3):
+        for half in range(2):
+            third[half, m].wait_recv()
+            part[half, m] = part[half, m] + rf[half, 0, m].astype(F32)
+            far_sum(half, m, 1)
+
+    for copy in pc_copies:
+        copy.wait_recv()
+    back_queries(0, W_EARLY)
+    exchange(0, 0, query_part)
+    heads_queries(1)
     heads_send(1)
-    for half in range(2):
-        third[half].wait_recv()
-        gath[B_EARLY, half, :, y, zl] = (part[half] + rf[half, 1].astype(F32)).astype(BF)
-    gather_first(B_EARLY)
-    gather_end(W_EARLY)
-    gather_last(B_EARLY)
-    forward(0, W_EARLY)
-    back_queries(0, W_EARLY)
+
+    for m in range(3):
+        for half in range(2):
+            third[half, m].wait_recv()
+            total = part[half, m] + rf[half, 1, m].astype(F32)
+            gath[B_EARLY, half, m, y, zl] = total.astype(BF)
+        gather_first(B_EARLY, m)
     heads_end(1)
-    gather_end(B_EARLY)
-
-    second(0, B_EARLY)
-    back_rest(0, W_EARLY, B_EARLY)
-    exchange(0)
+    for m in range(3):
+        gather_last(B_EARLY, m)
+    heads_queries(0)
+    for m in range(3):
+        gather_end(B_EARLY + m)
+        sides(0, B_EARLY, m)
+
+    second(0)
+    back_sides(0, B_EARLY)
+    back_rest(0, W_EARLY)
+    exchange(0, 1, rest_part)
     heads_send(0)
     heads_end(0)
 
@@ -465,11 +493,13 @@
         pltpu.VMEM((2, 2, 3, 16, 256), BF),
         pltpu.VMEM((2, T, 3 * DH), BF),
         pltpu.VMEM((2, T, 3 * DH), BF),
+        pltpu.VMEM((2, T, DH), F32),
+        pltpu.VMEM((4, T, DH), F32),
         pltpu.VMEM((2, 3, T, DH), BF),
         pltpu.VMEM((2, 3, T, DH), BF),
         dma((9,)),
     ]
-    for shape in ((2, 7), (2, 4), (4, 2, 3), (4, 2, 3), (2, 3, 3), (2, 3), (2, 2), (6,), (2, 3)):
+    for shape in ((2, 7), (3, 4), (6, 2, 3), (6, 2, 3), (2, 3, 3), (2, 3, 3), (2, 2, 3), (4,), (2, 2), (2, 3)):
         scratch += [dma(shape), dma(shape)]
     return pl.pallas_call(
         kernel,

time: 88.7 us -> 88.8 us (level)
  no operation moved by 1% of the time
where the time goes in v3:
time: 88.8 us; the launch traced here: 88.6 us
  Pallas kernels  86.3 us (97%)
  local copies, waits for them, and re-layouts  1.67 us (2%)
    pallas_call x1, Pallas kernels, local(): pl.pallas_call(kernel, name='meta_gradient', out_shape=jax.ShapeDtypeStru...  86.3 us

profile of v3, /device:TPU:1, one launch (start us, length us, event | category | flops | bytes accessed | tf_op | source)
XLA Modules:
  0.0 88.6 jit_solution(2512693528083175298)
XLA Ops:
  0.7 86.3 %meta_gradient.1 = bf16[2,256,256]{2,1,0:T(8,128)(2,1)} custom-call(bf16[2,256,256]{2,1,0:T(8,128)(2,1)} %xin.1, bf16[2048,256]{1,0:T(8,128)(2,1)} %pq.1, bf16[2048,256]{1,0:T(8,128)(2,1)} %pk.1, bf16[2048,256]{1,0:T(8,128)(2,1)} %pv.1, bf16[2,3,4,512]{3,2,1,0:T(4,128)(2,1)} %bitcast.2, bf16[2,256,256]{2,1,0:T(8,128)(2,1)} %og.1, f32[3,4,512]{2,1,0:T(4,128)} %bitcast.3, ...), custom_call_target="tpu_custom_call" | custom-call | tf_op jit(solution)/shard_map/meta_gradient/pallas_call | solution.py:504
  87.0 1.7 %copy.11 = bf16[2,256,256]{2,1,0:T(8,128)(2,1)} copy(bf16[2,256,256]{2,1,0:T(8,128)(2,1)} %meta_gradient.1) | data formatting | bytes 524288

commit v4 on v3

--- a/solution.py
+++ b/solution.py
@@ -26,10 +26,6 @@
     return lax.dot_general(a, b, (((1,), (1,)), ((), ())), preferred_element_type=F32)
 
 
-def t_mm(a, b):
-    return lax.dot_general(a, b, (((0,), (0,)), ((), ())), preferred_element_type=F32)
-
-
 def permutation():
     row = lax.broadcasted_iota(jnp.int32, (DH, DH), 0)
     place = lax.broadcasted_iota(jnp.int32, (DH, DH), 1)
@@ -40,7 +36,7 @@
 def kernel(
     xin, pq, pk, pv, ck, og, adj, rate, out,
     xg, pr, pc, pp, gath, fb, adjv, tile, ogv, qkv, o_s, fw, hb, own, rsend,
-    r1, acc, sd, r2, part, fsend, rf, gcat, gp, back, base, pb, ro,
+    turned, r1, acc, sd, r2, part, fsend, rf, gcat, gp, back, base, pb, ro,
     ls, xs, xr, fs, fr, as_, ar, bs, br, r1s, r1r, r2s, r2r, rfs, rfr, cs, cr, ps, pr_, hs, hr,
 ):
     z, y = lax.axis_index("z"), lax.axis_index("y")
@@ -52,6 +48,8 @@
         )
 
     zh, zl = z // 4, lax.rem(z, 4)
+    odd, pair_row = lax.rem(zh, 2), zh // 2
+    flip = 4 - 8 * odd
     skip = 4 * c - 2
     near = [1, -1, skip]
 
@@ -76,9 +74,9 @@
     loads = [
         pltpu.make_async_copy(src, dst, ls.at[i])
         for i, (src, dst) in enumerate((
-            (ck.at[1], fb.at[W_LATE, zh]),
+            (ck.at[1], fb.at[W_LATE, odd]),
             (adj, adjv),
-            (ck.at[0], fb.at[W_EARLY, zh]),
+            (ck.at[0], fb.at[W_EARLY, odd]),
             (xin.at[1], xg.at[1, :, pl.ds(column, DH)]),
             (pq, pr.at[0]),
             (pk, pr.at[1]),
@@ -89,29 +87,12 @@
     ]
     for load in loads:
         load.start()
-    for load in loads[:4]:
-        load.wait()
-    fb[B_LATE, zh] = adjv[...].astype(BF)
-
     pl.semaphore_wait(barrier, len(partners))
 
-    far_copies = {}
-
-    def far_send(i):
-        piece = fb.at[i, zh]
-        far_copies[i] = [
-            send(piece, piece, fs.at[i, n], fr.at[i, n], dev(dz=d)) for n, d in enumerate((4, -4))
-        ]
-
-    def far_relay(i):
-        for copy in far_copies[i]:
-            copy.wait_recv()
-        below = fb.at[i, lax.rem(zh + 3, 4), pl.ds(0, 1)]
-        above = fb.at[i, lax.rem(zh + 1, 4), pl.ds(1, 2)]
-        far_copies[i] = [
-            send(below, below, fs.at[i, 2], fr.at[i, 2], dev(dz=4)),
-            send(above, above, fs.at[i, 3], fr.at[i, 3], dev(dz=-4)),
-        ]
+    far_one, far_two = {}, {}
+
+    def far_send(s, piece):
+        far_one[s] = send(piece, fb.at[s, odd], fs.at[s, 0], fr.at[s, 0], dev(dz=flip))
 
     x_copies = {}
 
@@ -122,11 +103,13 @@
         ]
         x_copies[s].append(send(xin.at[s], block, xs.at[s, 3], xr.at[s, 3], dev(dc=1)))
 
-    far_send(W_LATE)
-    far_send(B_LATE)
+    far_send(W_LATE, ck.at[1])
+    loads[1].wait()
+    fb[B_LATE, odd] = adjv[...].astype(BF)
+    far_send(B_LATE, fb.at[B_LATE, odd])
     x_send(1)
-    far_send(W_EARLY)
-    x_send(0)
+    for i in (0, 2, 3):
+        loads[i].wait()
 
     order = permutation()
     for i in range(3):
@@ -135,21 +118,26 @@
             rows = pl.ds(j * DH, DH)
             pc[rows, pl.ds(i * DH, DH)] = mm(pr[i, rows, :], order).astype(BF)
 
-    far_relay(W_LATE)
-    far_relay(B_LATE)
-    far_relay(W_EARLY)
+    def rows8(of):
+        return pl.ds(pl.multiple_of(8 * of, 8), 8)
+
+    def assemble(s):
+        far_one[s].wait_recv()
+        for m in range(3):
+            for k in range(2):
+                tile[m, pl.ds(4 * k, 4), :] = fb[s, k, m].astype(F32)
+        for half in range(2):
+            rows = tile[:, :, pl.ds(half * 256, 256)].astype(BF)
+            for k in range(2):
+
+                @pl.when(pair_row == k)
+                def _():
+                    gath[s, half, :, y, zl, pl.ds(8 * k, 8), :] = rows
+
+        block = gath.at[s, :, :, y, zl, rows8(pair_row), :]
+        far_two[s] = send(block, block, fs.at[s, 1], fr.at[s, 1], dev(dz=-flip))
 
     other = 1 - c
-    pc_copies = []
-    for i in range(4):
-        rows = pl.multiple_of((i * 2 + other) * DH, DH)
-        pc_copies.append(
-            send(pc.at[pl.ds(rows, DH), :], pp.at[i], cs.at[i], cr.at[i], dev(dc=1))
-        )
-    loads[7].wait()
-    for s in range(2):
-        o_s[s] = mm(ogv[s], order).astype(BF)
-
     first, last = {}, {}
 
     def to_near(block, ssem, rsem):
@@ -158,36 +146,42 @@
     def to_y(block, ssem, rsem):
         return [send(block, block, ssem.at[i], rsem.at[i], dev(dy=d)) for i, d in enumerate((2, 1, 3))]
 
-    def gather_first(s, m=None):
-        index = s if m is None else s + m
-        mats = pl.ds(0, 3) if m is None else m
-        first[index] = []
-        for half, stage in ((0, to_near), (1, to_y)):
-            block = gath.at[s, half, mats, y, zl]
-            first[index] += stage(block, as_.at[index, half], ar.at[index, half])
-
-    def gather_last(s, m=None):
-        index = s if m is None else s + m
-        mats = pl.ds(0, 3) if m is None else m
+    members = [z] + [lax.rem(z + d + NZ, NZ) for d in (1, -1, -skip)]
+
+    def part_first(s, late):
+        if late:
+            far_two[s].wait_recv()
+        index = 2 * s + late
+        rows = rows8(1 - pair_row if late else pair_row)
+        first[index] = to_near(gath.at[s, 0, :, y, zl, rows, :], as_.at[index, 0], ar.at[index, 0])
+        first[index] += to_y(gath.at[s, 1, :, y, zl, rows, :], as_.at[index, 1], ar.at[index, 1])
+
+    def part_last(s, late):
+        index = 2 * s + late
         for copy in first[index]:
             copy.wait_recv()
-        last[index] = to_y(gath.at[s, 0, mats, y], bs.at[index, 0], br.at[index, 0])
-        last[index] += to_near(gath.at[s, 1, mats, :, zl], bs.at[index, 1], br.at[index, 1])
+        last[index] = []
+        for n, member in enumerate(members):
+            of = member // 8
+            block = gath.at[s, 0, :, y, lax.rem(member, 4), rows8(1 - of if late else of), :]
+            last[index] += to_y(block, bs.at[index, n], br.at[index, n])
+        block = gath.at[s, 1, :, :, zl, rows8(1 - pair_row if late else pair_row), :]
+        last[index] += to_near(block, bs.at[index, 4], br.at[index, 4])
+
+    def whole_first(s):
+        first[6] = to_near(gath.at[s, 0, :, y, zl], as_.at[6, 0], ar.at[6, 0])
+        first[6] += to_y(gath.at[s, 1, :, y, zl], as_.at[6, 1], ar.at[6, 1])
+
+    def whole_last(s):
+        for copy in first[6]:
+            copy.wait_recv()
+        last[6] = to_y(gath.at[s, 0, :, y], bs.at[6, 0], br.at[6, 0])
+        last[6] += to_near(gath.at[s, 1, :, :, zl], bs.at[6, 4], br.at[6, 4])
 
     def gather_end(s):
-        for copy in last[s]:
-            copy.wait_recv()
-
-    def far_end(i):
-        for copy in far_copies[i]:
-            copy.wait_recv()
-
-    def assemble(s):
-        for m in range(3):
-            for k in range(4):
-                tile[m, pl.ds(4 * k, 4), :] = fb[s, k, m].astype(F32)
-            gath[s, 0, m, y, zl] = tile[m, :, pl.ds(0, 256)].astype(BF)
-            gath[s, 1, m, y, zl] = tile[m, :, pl.ds(256, 256)].astype(BF)
+        for index in (6,) if s == B_EARLY else (2 * s, 2 * s + 1):
+            for copy in last[index]:
+                copy.wait_recv()
 
     relays = {}
 
@@ -321,36 +315,53 @@
             total = total + ro[s, i].astype(F32)
         out[s] = total.astype(BF)
 
+    assemble(W_LATE)
+    part_first(W_LATE, 0)
+    assemble(B_LATE)
+    part_first(B_LATE, 0)
+    far_send(W_EARLY, ck.at[0])
+    x_send(0)
+    pc_copies = []
+    for i in range(4):
+        rows = pl.multiple_of((i * 2 + other) * DH, DH)
+        pc_copies.append(
+            send(pc.at[pl.ds(rows, DH), :], pp.at[i], cs.at[i], cr.at[i], dev(dc=1))
+        )
+    loads[7].wait()
+    for s in range(2):
+        o_s[s] = mm(ogv[s], order).astype(BF)
+    part_last(W_LATE, 0)
+    part_first(W_LATE, 1)
+    part_first(B_LATE, 1)
+    part_last(B_LATE, 0)
     x_relay(1)
-    for s in (W_LATE, B_LATE, W_EARLY):
-        far_end(s)
-        assemble(s)
-        gather_first(s)
+    assemble(W_EARLY)
+    part_first(W_EARLY, 0)
     project(1)
-    gather_last(W_LATE)
-    gather_last(B_LATE)
+    part_last(W_LATE, 1)
+    part_last(B_LATE, 1)
+    part_first(W_EARLY, 1)
+    for i, rows in enumerate((qkv[1, 1], qkv[1, 0], qkv[1, 2], o_s[1])):
+        turned[i] = rows.T
     x_relay(0)
     loads[8].wait()
     project(0)
     gather_end(W_LATE)
-    gather_last(W_EARLY)
+    part_last(W_EARLY, 0)
     forward(1, W_LATE)
     back_queries(1, W_LATE)
+    part_last(W_EARLY, 1)
     gather_end(B_LATE)
     for m in range(3):
         sides(1, B_LATE, m)
     second(1)
 
-    terms = (
-        (qkv[1, 1], 3, qkv[1, 0], 1),
-        (qkv[1, 1], 4, qkv[1, 0], 2),
-        (qkv[1, 2], 5, o_s[1], 0),
-    )
+    terms = ((0, 3, 1, 1), (0, 4, 1, 2), (2, 5, 3, 0))
     sum_a, sum_b = {}, {}
     for m, (left, i, right, j) in enumerate(terms):
         for half in range(2):
             lanes = pl.ds(half * 256, 256)
-            grad = t_mm(left, hb[1, i, :, lanes]) + t_mm(right, hb[1, j, :, lanes])
+            grad = mm(turned[left], hb[1, i, :, lanes]) + mm(turned[right], hb[1, j, :, lanes])
             grad = grad.reshape(4, 4, 16, 256)
             own[half, m] = grad
             rsend[half, m] = grad.astype(BF)
@@ -370,7 +381,6 @@
     back_rest(1, W_LATE)
     exchange(1, 1, rest_part)
 
-    two = {}
     for m in range(3):
         for copy in sum_a[m]:
             copy.wait_recv()
@@ -379,11 +389,11 @@
             total = total + r1[0, m, i].astype(F32)
         acc[0, m] = total
         sd[0, m] = total.astype(BF)
-        two[0, m] = [
-            send(sd.at[0, m, lax.rem(z + d + NZ, 4)], r2.at[0, m, n],
-                 r2s.at[0, m, n], r2r.at[0, m, n], dev(dz=d))
-            for n, d in enumerate(near)
-        ]
+    two_a = [
+        send(sd.at[0, :, lax.rem(z + d + NZ, 4)], r2.at[0, n], r2s.at[0, n], r2r.at[0, n], dev(dz=d))
+        for n, d in enumerate(near)
+    ]
+    for m in range(3):
         for copy in sum_b[m]:
             copy.wait_recv()
         total = own[1, m, :, zl]
@@ -391,47 +401,43 @@
             total = total + r1[1, m, i].astype(F32)
         acc[1, m] = total
         sd[1, m] = total.astype(BF)
-        two[1, m] = [
-            send(sd.at[1, m, lax.rem(y + d, NY)], r2.at[1, m, n],
-                 r2s.at[1, m, n], r2r.at[1, m, n], dev(dy=d))
-            for n, d in enumerate((2, 1, 3))
-        ]
-
-    flip = 4 - 8 * lax.rem(zh, 2)
+    two_b = [
+        send(sd.at[1, :, lax.rem(y + d, NY)], r2.at[1, n], r2s.at[1, n], r2r.at[1, n], dev(dy=d))
+        for n, d in enumerate((2, 1, 3))
+    ]
+
     third = {}
 
-    def far_sum(half, m, step):
-        fsend[half, step, m] = part[half, m].astype(BF)
+    def far_sum(half, step):
+        fsend[half, step] = part[half].astype(BF)
         way = flip if half == step else -flip
-        third[half, m] = send(
-            fsend.at[half, step, m], rf.at[half, step, m],
-            rfs.at[half, step, m], rfr.at[half, step, m], dev(dz=way)
+        third[half] = send(
+            fsend.at[half, step], rf.at[half, step], rfs.at[half, step], rfr.at[half, step], dev(dz=way)
         )
 
-    for m in range(3):
-        for half, place in ((0, zl), (1, y)):
-            for copy in two[half, m]:
-                copy.wait_recv()
-            total = acc[half, m, place]
-            for i in range(3):
-                total = total + r2[half, m, i].astype(F32)
-            part[half, m] = total
-            for k in range(4):
-                mine = jnp.where(zh == k, 1.0, 0.0)
+    for half, copies, place in ((0, two_a, zl), (1, two_b, y)):
+        for copy in copies:
+            copy.wait_recv()
+        total = acc[half, :, place]
+        for i in range(3):
+            total = total + r2[half, i].astype(F32)
+        part[half] = total
+        for k in range(4):
+            mine = jnp.where(zh == k, 1.0, 0.0)
+            for m in range(3):
                 rows = pl.ds(4 * k, 4)
                 part[half, m, rows, :] = (
                     part[half, m, rows, :] + mine * adjv[m, :, pl.ds(half * 256, 256)]
                 )
-            far_sum(half, m, 0)
+        far_sum(half, 0)
 
     gather_end(W_EARLY)
     forward(0, W_EARLY)
 
-    for m in range(3):
-        for half in range(2):
-            third[half, m].wait_recv()
-            part[half, m] = part[half, m] + rf[half, 0, m].astype(F32)
-            far_sum(half, m, 1)
+    for half in range(2):
+        third[half].wait_recv()
+        part[half] = part[half] + rf[half, 0].astype(F32)
+        far_sum(half, 1)
 
     for copy in pc_copies:
         copy.wait_recv()
@@ -440,18 +446,15 @@
     heads_queries(1)
     heads_send(1)
 
+    for half in range(2):
+        third[half].wait_recv()
+        gath[B_EARLY, half, :, y, zl] = (part[half] + rf[half, 1].astype(F32)).astype(BF)
+    whole_first(B_EARLY)
+    heads_end(1)
+    whole_last(B_EARLY)
+    heads_queries(0)
+    gather_end(B_EARLY)
     for m in range(3):
-        for half in range(2):
-            third[half, m].wait_recv()
-            total = part[half, m] + rf[half, 1, m].astype(F32)
-            gath[B_EARLY, half, m, y, zl] = total.astype(BF)
-        gather_first(B_EARLY, m)
-    heads_end(1)
-    for m in range(3):
-        gather_last(B_EARLY, m)
-    heads_queries(0)
-    for m in range(3):
-        gather_end(B_EARLY + m)
         sides(0, B_EARLY, m)
 
     second(0)
@@ -474,9 +477,9 @@
         pltpu.VMEM((D, 3 * DH), BF),
         pltpu.VMEM((4, DH, 3 * DH), BF),
         pltpu.VMEM((4, 2, 3, 4, 4, 16, 256), BF),
-        pltpu.VMEM((3, 4, 3, 4, F), BF),
+        pltpu.VMEM((3, 2, 3, 4, F), BF),
         pltpu.VMEM((3, 4, F), F32),
-        pltpu.VMEM((3, 16, F), F32),
+        pltpu.VMEM((3, 8, F), F32),
         pltpu.VMEM((2, T, DH), BF),
         pltpu.VMEM((2, 3, T, DH), BF),
         pltpu.VMEM((2, T, DH), BF),
@@ -484,6 +487,7 @@
         pltpu.VMEM((2, 9, T, F), BF),
         pltpu.VMEM((2, 3, 4, 4, 16, 256), F32),
         pltpu.VMEM((2, 3, 4, 4, 16, 256), BF),
+        pltpu.VMEM((4, DH, T), BF),
         pltpu.VMEM((2, 3, 3, 4, 16, 256), BF),
         pltpu.VMEM((2, 3, 4, 16, 256), F32),
         pltpu.VMEM((2, 3, 4, 16, 256), BF),
@@ -499,7 +503,7 @@
         pltpu.VMEM((2, 3, T, DH), BF),
         dma((9,)),
     ]
-    for shape in ((2, 7), (3, 4), (6, 2, 3), (6, 2, 3), (2, 3, 3), (2, 3, 3), (2, 2, 3), (4,), (2, 2), (2, 3)):
+    for shape in ((2, 7), (3, 2), (7, 2, 3), (7, 5, 3), (2, 3, 3), (2, 3), (2, 2), (4,), (2, 2), (2, 3)):
         scratch += [dma(shape), dma(shape)]
     return pl.pallas_call(
         kernel,

time: 88.8 us -> 92 us (1.036)
  Pallas kernels: 86.3 us -> 89.6 us
    pallas_call x1, Pallas kernels: 86.3 us -> 89.6 us  [local(): pl.pallas_call(kernel, name='meta_gradient', out_shape=jax.ShapeDtypeStru...]
where the time goes in v4:
time: 92 us; the launch traced here: 91.9 us
  Pallas kernels  89.6 us (97%)
  local copies, waits for them, and re-layouts  1.67 us (2%)
    pallas_call x1, Pallas kernels, local(): pl.pallas_call(kernel, name='meta_gradient', out_shape=jax.ShapeDtypeStru...  89.6 us

profile of v4, /device:TPU:1, one launch (start us, length us, event | category | flops | bytes accessed | tf_op | source)
XLA Modules:
  0.0 91.9 jit_solution(2849864418250375558)
XLA Ops:
  0.7 89.6 %meta_gradient.1 = bf16[2,256,256]{2,1,0:T(8,128)(2,1)} custom-call(bf16[2,256,256]{2,1,0:T(8,128)(2,1)} %xin.1, bf16[2048,256]{1,0:T(8,128)(2,1)} %pq.1, bf16[2048,256]{1,0:T(8,128)(2,1)} %pk.1, bf16[2048,256]{1,0:T(8,128)(2,1)} %pv.1, bf16[2,3,4,512]{3,2,1,0:T(4,128)(2,1)} %bitcast.2, bf16[2,256,256]{2,1,0:T(8,128)(2,1)} %og.1, f32[3,4,512]{2,1,0:T(4,128)} %bitcast.3, ...), custom_call_target="tpu_custom_call" | custom-call | tf_op jit(solution)/shard_map/meta_gradient/pallas_call | solution.py:508
  90.2 1.7 %copy.11 = bf16[2,256,256]{2,1,0:T(8,128)(2,1)} copy(bf16[2,256,256]{2,1,0:T(8,128)(2,1)} %meta_gradient.1) | data formatting | bytes 524288

commit v5 on v4

--- a/solution.py
+++ b/solution.py
@@ -16,6 +16,7 @@
 F = 512
 D = 2048
 W_LATE, B_LATE, W_EARLY, B_EARLY = 0, 1, 2, 3
+SPLIT = (3, 3, 3, 4)
 
 
 def mm(a, b):
@@ -51,7 +52,7 @@
     odd, pair_row = lax.rem(zh, 2), zh // 2
     flip = 4 - 8 * odd
     skip = 4 * c - 2
-    near = [1, -1, skip]
+    near = [skip, 1, -1]
 
     barrier = pltpu.get_barrier_semaphore()
     partners = [dev(dz=d) for d in (4, -4, 2, -2, 1, -1)]
@@ -132,9 +133,9 @@
 
                 @pl.when(pair_row == k)
                 def _():
-                    gath[s, half, :, y, zl, pl.ds(8 * k, 8), :] = rows
-
-        block = gath.at[s, :, :, y, zl, rows8(pair_row), :]
+                    gath[s, pl.ds(3 * half, 3), y, zl, pl.ds(8 * k, 8), :] = rows
+
+        block = gath.at[s, :, y, zl, rows8(pair_row), :]
         far_two[s] = send(block, block, fs.at[s, 1], fr.at[s, 1], dev(dz=-flip))
 
     other = 1 - c
@@ -146,42 +147,23 @@
     def to_y(block, ssem, rsem):
         return [send(block, block, ssem.at[i], rsem.at[i], dev(dy=d)) for i, d in enumerate((2, 1, 3))]
 
-    members = [z] + [lax.rem(z + d + NZ, NZ) for d in (1, -1, -skip)]
-
-    def part_first(s, late):
-        if late:
+    def gather_first(s):
+        if s != B_EARLY:
             far_two[s].wait_recv()
-        index = 2 * s + late
-        rows = rows8(1 - pair_row if late else pair_row)
-        first[index] = to_near(gath.at[s, 0, :, y, zl, rows, :], as_.at[index, 0], ar.at[index, 0])
-        first[index] += to_y(gath.at[s, 1, :, y, zl, rows, :], as_.at[index, 1], ar.at[index, 1])
-
-    def part_last(s, late):
-        index = 2 * s + late
-        for copy in first[index]:
+        a, b = pl.ds(0, SPLIT[s]), pl.ds(SPLIT[s], 6 - SPLIT[s])
+        first[s] = to_near(gath.at[s, a, y, zl], as_.at[s, 0], ar.at[s, 0])
+        first[s] += to_y(gath.at[s, b, y, zl], as_.at[s, 1], ar.at[s, 1])
+
+    def gather_last(s):
+        for copy in first[s]:
             copy.wait_recv()
-        last[index] = []
-        for n, member in enumerate(members):
-            of = member // 8
-            block = gath.at[s, 0, :, y, lax.rem(member, 4), rows8(1 - of if late else of), :]
-            last[index] += to_y(block, bs.at[index, n], br.at[index, n])
-        block = gath.at[s, 1, :, :, zl, rows8(1 - pair_row if late else pair_row), :]
-        last[index] += to_near(block, bs.at[index, 4], br.at[index, 4])
-
-    def whole_first(s):
-        first[6] = to_near(gath.at[s, 0, :, y, zl], as_.at[6, 0], ar.at[6, 0])
-        first[6] += to_y(gath.at[s, 1, :, y, zl], as_.at[6, 1], ar.at[6, 1])
-
-    def whole_last(s):
-        for copy in first[6]:
+        a, b = pl.ds(0, SPLIT[s]), pl.ds(SPLIT[s], 6 - SPLIT[s])
+        last[s] = to_y(gath.at[s, a, y], bs.at[s, 0], br.at[s, 0])
+        last[s] += to_near(gath.at[s, b, :, zl], bs.at[s, 1], br.at[s, 1])
+
+    def gather_end(s):
+        for copy in last[s]:
             copy.wait_recv()
-        last[6] = to_y(gath.at[s, 0, :, y], bs.at[6, 0], br.at[6, 0])
-        last[6] += to_near(gath.at[s, 1, :, :, zl], bs.at[6, 4], br.at[6, 4])
-
-    def gather_end(s):
-        for index in (6,) if s == B_EARLY else (2 * s, 2 * s + 1):
-            for copy in last[index]:
-                copy.wait_recv()
 
     relays = {}
 
@@ -202,7 +184,7 @@
     factor = rate[0] / 16384.0
 
     def weight(s, half, m):
-        return gath[s, half, m].reshape(DH, 256)
+        return gath[s, 3 * half + m].reshape(DH, 256)
 
     def ahead(rows, s, m, to):
         for half in range(2):
@@ -316,9 +298,7 @@
         out[s] = total.astype(BF)
 
     assemble(W_LATE)
-    part_first(W_LATE, 0)
     assemble(B_LATE)
-    part_first(B_LATE, 0)
     far_send(W_EARLY, ck.at[0])
     x_send(0)
     pc_copies = []
@@ -330,104 +310,102 @@
     loads[7].wait()
     for s in range(2):
         o_s[s] = mm(ogv[s], order).astype(BF)
-    part_last(W_LATE, 0)
-    part_first(W_LATE, 1)
-    part_first(B_LATE, 1)
-    part_last(B_LATE, 0)
     x_relay(1)
+    gather_first(W_LATE)
+    gather_first(B_LATE)
     assemble(W_EARLY)
-    part_first(W_EARLY, 0)
     project(1)
-    part_last(W_LATE, 1)
-    part_last(B_LATE, 1)
-    part_first(W_EARLY, 1)
+    gather_last(W_LATE)
+    gather_last(B_LATE)
+    gather_first(W_EARLY)
     for i, rows in enumerate((qkv[1, 1], qkv[1, 0], qkv[1, 2], o_s[1])):
         turned[i] = rows.T
     x_relay(0)
     loads[8].wait()
     project(0)
     gather_end(W_LATE)
-    part_last(W_EARLY, 0)
+    gather_last(W_EARLY)
     forward(1, W_LATE)
     back_queries(1, W_LATE)
-    part_last(W_EARLY, 1)
     gather_end(B_LATE)
     for m in range(3):
         sides(1, B_LATE, m)
     second(1)
 
     terms = ((0, 3, 1, 1), (0, 4, 1, 2), (2, 5, 3, 0))
-    sum_a, sum_b = {}, {}
+    split = SPLIT[B_EARLY]
+    sums = {}
     for m, (left, i, right, j) in enumerate(terms):
         for half in range(2):
             lanes = pl.ds(half * 256, 256)
+            h = 3 * half + m
             grad = mm(turned[left], hb[1, i, :, lanes]) + mm(turned[right], hb[1, j, :, lanes])
             grad = grad.reshape(4, 4, 16, 256)
-            own[half, m] = grad
-            rsend[half, m] = grad.astype(BF)
-        sum_a[m] = [
-            send(rsend.at[0, m, lax.rem(y + d, NY)], r1.at[0, m, n],
-                 r1s.at[0, m, n], r1r.at[0, m, n], dev(dy=d))
-            for n, d in enumerate((2, 1, 3))
-        ]
-        sum_b[m] = [
-            send(rsend.at[1, m, :, lax.rem(z + d + NZ, 4)], r1.at[1, m, n],
-                 r1s.at[1, m, n], r1r.at[1, m, n], dev(dz=d))
-            for n, d in enumerate(near)
-        ]
+            own[h] = grad
+            rsend[h] = grad.astype(BF)
+            if h < split:
+                sums[h] = [
+                    send(rsend.at[h, lax.rem(y + d, NY)], r1.at[h, n],
+                         r1s.at[h, n], r1r.at[h, n], dev(dy=d))
+                    for n, d in enumerate((2, 1, 3))
+                ]
+            else:
+                sums[h] = [
+                    send(rsend.at[h, :, lax.rem(z + d + NZ, 4)], r1.at[h, n],
+                         r1s.at[h, n], r1r.at[h, n], dev(dz=d))
+                    for n, d in enumerate(near)
+                ]
 
     exchange(1, 0, query_part)
     back_sides(1, B_LATE)
     back_rest(1, W_LATE)
     exchange(1, 1, rest_part)
 
-    for m in range(3):
-        for copy in sum_a[m]:
+    def first_sum(h):
+        for copy in sums[h]:
             copy.wait_recv()
-        total = own[0, m, y]
+        total = own[h, y] if h < split else own[h, :, zl]
         for i in range(3):
-            total = total + r1[0, m, i].astype(F32)
-        acc[0, m] = total
-        sd[0, m] = total.astype(BF)
+            total = total + r1[h, i].astype(F32)
+        acc[h] = total
+        sd[h] = total.astype(BF)
+
+    a, b = pl.ds(0, split), pl.ds(split, 6 - split)
+    for h in range(split):
+        first_sum(h)
     two_a = [
-        send(sd.at[0, :, lax.rem(z + d + NZ, 4)], r2.at[0, n], r2s.at[0, n], r2r.at[0, n], dev(dz=d))
+        send(sd.at[a, lax.rem(z + d + NZ, 4)], r2.at[n, a], r2s.at[0, n], r2r.at[0, n], dev(dz=d))
         for n, d in enumerate(near)
     ]
-    for m in range(3):
-        for copy in sum_b[m]:
-            copy.wait_recv()
-        total = own[1, m, :, zl]
-        for i in range(3):
-            total = total + r1[1, m, i].astype(F32)
-        acc[1, m] = total
-        sd[1, m] = total.astype(BF)
+    for h in range(split, 6):
+        first_sum(h)
     two_b = [
-        send(sd.at[1, :, lax.rem(y + d, NY)], r2.at[1, n], r2s.at[1, n], r2r.at[1, n], dev(dy=d))
+        send(sd.at[b, lax.rem(y + d, NY)], r2.at[n, b], r2s.at[1, n], r2r.at[1, n], dev(dy=d))
         for n, d in enumerate((2, 1, 3))
     ]
 
     third = {}
 
     def far_sum(half, step):
-        fsend[half, step] = part[half].astype(BF)
+        fsend[half, step] = part[pl.ds(3 * half, 3)].astype(BF)
         way = flip if half == step else -flip
         third[half] = send(
             fsend.at[half, step], rf.at[half, step], rfs.at[half, step], rfr.at[half, step], dev(dz=way)
         )
 
-    for half, copies, place in ((0, two_a, zl), (1, two_b, y)):
+    for half, copies, place, span_of in ((0, two_a, zl, range(split)), (1, two_b, y, range(split, 6))):
         for copy in copies:
             copy.wait_recv()
-        total = acc[half, :, place]
-        for i in range(3):
-            total = total + r2[half, i].astype(F32)
-        part[half] = total
-        for k in range(4):
-            mine = jnp.where(zh == k, 1.0, 0.0)
-            for m in range(3):
+        for h in span_of:
+            total = acc[h, place]
+            for i in range(3):
+                total = total + r2[i, h].astype(F32)
+            part[h] = total
+            for k in range(4):
+                mine = jnp.where(zh == k, 1.0, 0.0)
                 rows = pl.ds(4 * k, 4)
-                part[half, m, rows, :] = (
-                    part[half, m, rows, :] + mine * adjv[m, :, pl.ds(half * 256, 256)]
+                part[h, rows, :] = (
+                    part[h, rows, :] + mine * adjv[h % 3, :, pl.ds(h // 3 * 256, 256)]
                 )
         far_sum(half, 0)
 
@@ -436,7 +414,7 @@
 
     for half in range(2):
         third[half].wait_recv()
-        part[half] = part[half] + rf[half, 0].astype(F32)
+        part[pl.ds(3 * half, 3)] = part[pl.ds(3 * half, 3)] + rf[half, 0].astype(F32)
         far_sum(half, 1)
 
     for copy in pc_copies:
@@ -448,10 +426,11 @@
 
     for half in range(2):
         third[half].wait_recv()
-        gath[B_EARLY, half, :, y, zl] = (part[half] + rf[half, 1].astype(F32)).astype(BF)
-    whole_first(B_EARLY)
+        total = part[pl.ds(3 * half, 3)] + rf[half, 1].astype(F32)
+        gath[B_EARLY, pl.ds(3 * half, 3), y, zl] = total.astype(BF)
+    gather_first(B_EARLY)
+    gather_last(B_EARLY)
     heads_end(1)
-    whole_last(B_EARLY)
     heads_queries(0)
     gather_end(B_EARLY)
     for m in range(3):
@@ -476,7 +455,7 @@
         pltpu.VMEM((3, D, DH), BF),
         pltpu.VMEM((D, 3 * DH), BF),
         pltpu.VMEM((4, DH, 3 * DH), BF),
-        pltpu.VMEM((4, 2, 3, 4, 4, 16, 256), BF),
+        pltpu.VMEM((4, 6, 4, 4, 16, 256), BF),
         pltpu.VMEM((3, 2, 3, 4, F), BF),
         pltpu.VMEM((3, 4, F), F32),
         pltpu.VMEM((3, 8, F), F32),
@@ -485,14 +464,14 @@
         pltpu.VMEM((2, T, DH), BF),
         pltpu.VMEM((2, 9, T, F), F32),
         pltpu.VMEM((2, 9, T, F), BF),
-        pltpu.VMEM((2, 3, 4, 4, 16, 256), F32),
-        pltpu.VMEM((2, 3, 4, 4, 16, 256), BF),
+        pltpu.VMEM((6, 4, 4, 16, 256), F32),
+        pltpu.VMEM((6, 4, 4, 16, 256), BF),
         pltpu.VMEM((4, DH, T), BF),
-        pltpu.VMEM((2, 3, 3, 4, 16, 256), BF),
-        pltpu.VMEM((2, 3, 4, 16, 256), F32),
-        pltpu.VMEM((2, 3, 4, 16, 256), BF),
-        pltpu.VMEM((2, 3, 3, 16, 256), BF),
-        pltpu.VMEM((2, 3, 16, 256), F32),
+        pltpu.VMEM((6, 3, 4, 16, 256), BF),
+        pltpu.VMEM((6, 4, 16, 256), F32),
+        pltpu.VMEM((6, 4, 16, 256), BF),
+        pltpu.VMEM((3, 6, 16, 256), BF),
+        pltpu.VMEM((6, 16, 256), F32),
         pltpu.VMEM((2, 2, 3, 16, 256), BF),
         pltpu.VMEM((2, 2, 3, 16, 256), BF),
         pltpu.VMEM((2, T, 3 * DH), BF),
@@ -503,7 +482,7 @@
         pltpu.VMEM((2, 3, T, DH), BF),
         dma((9,)),
     ]
-    for shape in ((2, 7), (3, 2), (7, 2, 3), (7, 5, 3), (2, 3, 3), (2, 3), (2, 2), (4,), (2, 2), (2, 3)):
+    for shape in ((2, 7), (3, 2), (4, 2, 3), (4, 2, 3), (6, 3), (2, 3), (2, 2), (4,), (2, 2), (2, 3)):
         scratch += [dma(shape), dma(shape)]
     return pl.pallas_call(
         kernel,

time: 92 us -> 93.8 us (1.020)
  Pallas kernels: 89.6 us -> 91.3 us
    pallas_call x1, Pallas kernels: 89.6 us -> 91.3 us  [local(): pl.pallas_call(kernel, name='meta_gradient', out_shape=jax.ShapeDtypeStru...]
where the time goes in v5:
time: 93.8 us; the launch traced here: 93.7 us
  Pallas kernels  91.3 us (97%)
  local copies, waits for them, and re-layouts  1.67 us (2%)
    pallas_call x1, Pallas kernels, local(): pl.pallas_call(kernel, name='meta_gradient', out_shape=jax.ShapeDtypeStru...  91.3 us

profile of v5, /device:TPU:1, one launch (start us, length us, event | category | flops | bytes accessed | tf_op | source)
XLA Modules:
  0.0 93.7 jit_solution(10955031429733460176)
XLA Ops:
  0.7 91.3 %meta_gradient.1 = bf16[2,256,256]{2,1,0:T(8,128)(2,1)} custom-call(bf16[2,256,256]{2,1,0:T(8,128)(2,1)} %xin.1, bf16[2048,256]{1,0:T(8,128)(2,1)} %pq.1, bf16[2048,256]{1,0:T(8,128)(2,1)} %pk.1, bf16[2048,256]{1,0:T(8,128)(2,1)} %pv.1, bf16[2,3,4,512]{3,2,1,0:T(4,128)(2,1)} %bitcast.2, bf16[2,256,256]{2,1,0:T(8,128)(2,1)} %og.1, f32[3,4,512]{2,1,0:T(4,128)} %bitcast.3, ...), custom_call_target="tpu_custom_call" | custom-call | tf_op jit(solution)/shard_map/meta_gradient/pallas_call | solution.py:487
  92.0 1.7 %copy.11 = bf16[2,256,256]{2,1,0:T(8,128)(2,1)} copy(bf16[2,256,256]{2,1,0:T(8,128)(2,1)} %meta_gradient.1) | data formatting | bytes 524288

commit v6 on v5

--- a/solution.py
+++ b/solution.py
@@ -16,7 +16,7 @@
 F = 512
 D = 2048
 W_LATE, B_LATE, W_EARLY, B_EARLY = 0, 1, 2, 3
-SPLIT = (3, 3, 3, 4)
+SPLIT = (3, 3, 6, 3)
 
 
 def mm(a, b):
@@ -152,14 +152,16 @@
             far_two[s].wait_recv()
         a, b = pl.ds(0, SPLIT[s]), pl.ds(SPLIT[s], 6 - SPLIT[s])
         first[s] = to_near(gath.at[s, a, y, zl], as_.at[s, 0], ar.at[s, 0])
-        first[s] += to_y(gath.at[s, b, y, zl], as_.at[s, 1], ar.at[s, 1])
+        if SPLIT[s] < 6:
+            first[s] += to_y(gath.at[s, b, y, zl], as_.at[s, 1], ar.at[s, 1])
 
     def gather_last(s):
         for copy in first[s]:
             copy.wait_recv()
         a, b = pl.ds(0, SPLIT[s]), pl.ds(SPLIT[s], 6 - SPLIT[s])
         last[s] = to_y(gath.at[s, a, y], bs.at[s, 0], br.at[s, 0])
-        last[s] += to_near(gath.at[s, b, :, zl], bs.at[s, 1], br.at[s, 1])
+        if SPLIT[s] < 6:
+            last[s] += to_near(gath.at[s, b, :, zl], bs.at[s, 1], br.at[s, 1])
 
     def gather_end(s):
         for copy in last[s]:
@@ -313,20 +315,16 @@
     x_relay(1)
     gather_first(W_LATE)
     gather_first(B_LATE)
-    assemble(W_EARLY)
     project(1)
     gather_last(W_LATE)
     gather_last(B_LATE)
-    gather_first(W_EARLY)
+    assemble(W_EARLY)
     for i, rows in enumerate((qkv[1, 1], qkv[1, 0], qkv[1, 2], o_s[1])):
         turned[i] = rows.T
-    x_relay(0)
-    loads[8].wait()
-    project(0)
     gather_end(W_LATE)
-    gather_last(W_EARLY)
     forward(1, W_LATE)
     back_queries(1, W_LATE)
+    gather_first(W_EARLY)
     gather_end(B_LATE)
     for m in range(3):
         sides(1, B_LATE, m)
@@ -360,6 +358,7 @@
     back_sides(1, B_LATE)
     back_rest(1, W_LATE)
     exchange(1, 1, rest_part)
+    x_relay(0)
 
     def first_sum(h):
         for copy in sums[h]:
@@ -383,6 +382,9 @@
         send(sd.at[b, lax.rem(y + d, NY)], r2.at[n, b], r2s.at[1, n], r2r.at[1, n], dev(dy=d))
         for n, d in enumerate((2, 1, 3))
     ]
+
+    loads[8].wait()
+    project(0)
 
     third = {}
 
@@ -409,20 +411,16 @@
                 )
         far_sum(half, 0)
 
-    gather_end(W_EARLY)
-    forward(0, W_EARLY)
+    gather_last(W_EARLY)
+    for copy in pc_copies:
+        copy.wait_recv()
+    heads_queries(1)
+    heads_send(1)
 
     for half in range(2):
         third[half].wait_recv()
         part[pl.ds(3 * half, 3)] = part[pl.ds(3 * half, 3)] + rf[half, 0].astype(F32)
         far_sum(half, 1)
-
-    for copy in pc_copies:
-        copy.wait_recv()
-    back_queries(0, W_EARLY)
-    exchange(0, 0, query_part)
-    heads_queries(1)
-    heads_send(1)
 
     for half in range(2):
         third[half].wait_recv()
@@ -431,6 +429,10 @@
     gather_first(B_EARLY)
     gather_last(B_EARLY)
     heads_end(1)
+    gather_end(W_EARLY)
+    forward(0, W_EARLY)
+    back_queries(0, W_EARLY)
+    exchange(0, 0, query_part)
     heads_queries(0)
     gather_end(B_EARLY)
     for m in range(3):

time: 93.8 us -> 89.5 us (0.954)
  Pallas kernels: 91.3 us -> 87 us
    pallas_call x1, Pallas kernels: 91.3 us -> 87 us  [local(): pl.pallas_call(kernel, name='meta_gradient', out_shape=jax.ShapeDtypeStru...]
where the time goes in v6:
time: 89.5 us; the launch traced here: 89.3 us
  Pallas kernels  87 us (97%)
  local copies, waits for them, and re-layouts  1.67 us (2%)
    pallas_call x1, Pallas kernels, local(): pl.pallas_call(kernel, name='meta_gradient', out_shape=jax.ShapeDtypeStru...  87 us

profile of v6, /device:TPU:1, one launch (start us, length us, event | category | flops | bytes accessed | tf_op | source)
XLA Modules:
  0.0 89.3 jit_solution(5203058083157646289)
XLA Ops:
  0.7 87.0 %meta_gradient.1 = bf16[2,256,256]{2,1,0:T(8,128)(2,1)} custom-call(bf16[2,256,256]{2,1,0:T(8,128)(2,1)} %xin.1, bf16[2048,256]{1,0:T(8,128)(2,1)} %pq.1, bf16[2048,256]{1,0:T(8,128)(2,1)} %pk.1, bf16[2048,256]{1,0:T(8,128)(2,1)} %pv.1, bf16[2,3,4,512]{3,2,1,0:T(4,128)(2,1)} %bitcast.2, bf16[2,256,256]{2,1,0:T(8,128)(2,1)} %og.1, f32[3,4,512]{2,1,0:T(4,128)} %bitcast.3, ...), custom_call_target="tpu_custom_call" | custom-call | tf_op jit(solution)/shard_map/meta_gradient/pallas_call | solution.py:489
  87.7 1.7 %copy.11 = bf16[2,256,256]{2,1,0:T(8,128)(2,1)} copy(bf16[2,256,256]{2,1,0:T(8,128)(2,1)} %meta_gradient.1) | data formatting | bytes 524288

commit v7 on v2

--- a/solution.py
+++ b/solution.py
@@ -26,10 +26,6 @@
     return lax.dot_general(a, b, (((1,), (1,)), ((), ())), preferred_element_type=F32)
 
 
-def t_mm(a, b):
-    return lax.dot_general(a, b, (((0,), (0,)), ((), ())), preferred_element_type=F32)
-
-
 def permutation():
     row = lax.broadcasted_iota(jnp.int32, (DH, DH), 0)
     place = lax.broadcasted_iota(jnp.int32, (DH, DH), 1)
@@ -40,8 +36,8 @@
 def kernel(
     xin, pq, pk, pv, ck, og, adj, rate, out,
     xg, pr, pc, pp, gath, fb, adjv, tile, ogv, qkv, o_s, fw, hb, own, rsend,
-    r1, acc, sd, r2, part, fsend, rf, gcat, gp, pb, ro,
-    ls, xs, xr, fs, fr, as_, ar, bs, br, r1s, r1r, r2s, r2r, rfs, rfr, cs, cr, hs, hr,
+    turned, r1, acc, sd, r2, part, fsend, rf, gcat, gp, back, base, pb, ro,
+    ls, xs, xr, fs, fr, as_, ar, bs, br, r1s, r1r, r2s, r2r, rfs, rfr, cs, cr, ps, pr_, hs, hr,
 ):
     z, y = lax.axis_index("z"), lax.axis_index("y")
     x, c = lax.axis_index("x"), lax.axis_index("c")
@@ -255,11 +251,10 @@
             hb[s, 7, rows, :] = (e * us).astype(BF)
             hb[s, 8, rows, :] = (e * act).astype(BF)
 
-    def second(s, b):
-        ahead(qkv[s, 2], b, 2, (s, 6))
-        ahead(qkv[s, 1], b, 0, (s, 7))
-        ahead(qkv[s, 1], b, 1, (s, 8))
-
+    def sides(s, b, m):
+        ahead(qkv[s, 1] if m < 2 else qkv[s, 2], b, m, (s, (7, 8, 6)[m]))
+
+    def second(s):
         @pl.loop(0, T // 16)
         def _(step):
             rows = pl.ds(pl.multiple_of(step * 16, 16), 16)
@@ -273,39 +268,53 @@
         grad = behind(s, 1, w, 0) + behind(s, 2, w, 1)
         gcat[s, :, pl.ds(0, DH)] = grad.astype(BF)
 
-    def back_rest(s, w, b):
-        grad = behind(s, 3, w, 0) + behind(s, 4, w, 1)
-        grad = grad + behind(s, 7, b, 0) + behind(s, 8, b, 1)
+    def back_sides(s, b):
+        back[0] = behind(s, 7, b, 0) + behind(s, 8, b, 1)
+        back[1] = behind(s, 6, b, 2)
+
+    def back_rest(s, w):
+        grad = behind(s, 3, w, 0) + behind(s, 4, w, 1) + back[0]
         gcat[s, :, pl.ds(DH, DH)] = grad.astype(BF)
-        grad = behind(s, 5, w, 2) + behind(s, 6, b, 2)
+        grad = behind(s, 5, w, 2) + back[1]
         gcat[s, :, pl.ds(2 * DH, DH)] = grad.astype(BF)
 
     pair = {}
-
-    def exchange(s):
-        pair[s] = send(gcat.at[s], gp.at[s], cs.at[4 + s], cr.at[4 + s], dev(dc=1))
+    query_part, rest_part = pl.ds(0, DH), pl.ds(DH, 2 * DH)
+
+    def exchange(s, i, lanes):
+        pair[s, i] = send(
+            gcat.at[s, :, lanes], gp.at[s, :, lanes], ps.at[s, i], pr_.at[s, i], dev(dc=1)
+        )
 
     heads = {}
-
-    def partial_of(s, step):
-        to = lax.rem(x + step, NX)
-        rows = pl.multiple_of((to * 2 + c) * DH, DH)
-        return mm_t(gcat[s], pc[pl.ds(rows, DH), :]) + mm_t(gp[s], pp[to])
+    steps = (2, 1, 3, 0)
+
+    def own_term(s, step, lanes):
+        rows = pl.multiple_of((lax.rem(x + step, NX) * 2 + c) * DH, DH)
+        return mm_t(gcat[s, :, lanes], pc[pl.ds(rows, DH), lanes])
+
+    def pair_term(s, step, lanes):
+        return mm_t(gp[s, :, lanes], pp[lax.rem(x + step, NX), :, lanes])
+
+    def heads_queries(s):
+        pair[s, 0].wait_recv()
+        for i, step in enumerate(steps):
+            base[i] = own_term(s, step, query_part) + pair_term(s, step, query_part)
 
     def heads_send(s):
-        if s == 1:
-            for copy in pc_copies:
-                copy.wait_recv()
-        pair[s].wait_recv()
+        for i, step in enumerate(steps):
+            base[i] = base[i] + own_term(s, step, rest_part)
+        pair[s, 1].wait_recv()
         heads[s] = []
-        for i, step in enumerate((2, 1, 3)):
-            pb[s, i] = partial_of(s, step).astype(BF)
+        for i, step in enumerate(steps[:3]):
+            pb[s, i] = (base[i] + pair_term(s, step, rest_part)).astype(BF)
             heads[s].append(
                 send(pb.at[s, i], ro.at[s, i], hs.at[s, i], hr.at[s, i], dev(dx=step))
             )
+        base[3] = base[3] + pair_term(s, 0, rest_part)
 
     def heads_end(s):
-        total = partial_of(s, 0)
+        total = base[3]
         for i in range(3):
             heads[s][i].wait_recv()
             total = total + ro[s, i].astype(F32)
@@ -323,21 +332,21 @@
     assemble(W_EARLY)
     gather_first(W_EARLY)
     project(1)
+    for i, rows in enumerate((qkv[1, 1], qkv[1, 0], qkv[1, 2], o_s[1])):
+        turned[i] = rows.T
     gather_end(W_LATE)
     forward(1, W_LATE)
     gather_end(B_LATE)
-    second(1, B_LATE)
-
-    terms = (
-        (qkv[1, 1], 3, qkv[1, 0], 1),
-        (qkv[1, 1], 4, qkv[1, 0], 2),
-        (qkv[1, 2], 5, o_s[1], 0),
-    )
+    for m in range(3):
+        sides(1, B_LATE, m)
+    second(1)
+
+    terms = ((0, 3, 1, 1), (0, 4, 1, 2), (2, 5, 3, 0))
     sum_a, sum_b = {}, {}
     for m, (left, i, right, j) in enumerate(terms):
         for half in range(2):
             lanes = pl.ds(half * 256, 256)
-            grad = t_mm(left, hb[1, i, :, lanes]) + t_mm(right, hb[1, j, :, lanes])
+            grad = mm(turned[left], hb[1, i, :, lanes]) + mm(turned[right], hb[1, j, :, lanes])
             grad = grad.reshape(4, 4, 16, 256)
             own[half, m] = grad
             rsend[half, m] = grad.astype(BF)
@@ -353,8 +362,10 @@
         ]
 
     back_queries(1, W_LATE)
-    back_rest(1, W_LATE, B_LATE)
-    exchange(1)
+    exchange(1, 0, query_part)
+    back_sides(1, B_LATE)
+    back_rest(1, W_LATE)
+    exchange(1, 1, rest_part)
 
     for m in range(3):
         for copy in sum_a[m]:
@@ -364,6 +375,11 @@
             total = total + r1[0, m, i].astype(F32)
         acc[0, m] = total
         sd[0, m] = total.astype(BF)
+    two_a = [
+        send(sd.at[0, :, lax.rem(z + d + NZ, 4)], r2.at[0, n], r2s.at[0, n], r2r.at[0, n], dev(dz=d))
+        for n, d in enumerate(near)
+    ]
+    for m in range(3):
         for copy in sum_b[m]:
             copy.wait_recv()
         total = own[1, m, :, zl]
@@ -371,10 +387,6 @@
             total = total + r1[1, m, i].astype(F32)
         acc[1, m] = total
         sd[1, m] = total.astype(BF)
-    two_a = [
-        send(sd.at[0, :, lax.rem(z + d + NZ, 4)], r2.at[0, n], r2s.at[0, n], r2r.at[0, n], dev(dz=d))
-        for n, d in enumerate(near)
-    ]
     two_b = [
         send(sd.at[1, :, lax.rem(y + d, NY)], r2.at[1, n], r2s.at[1, n], r2r.at[1, n], dev(dy=d))
         for n, d in enumerate((2, 1, 3))
@@ -415,21 +427,29 @@
         third[half].wait_recv()
         part[half] = part[half] + rf[half, 0].astype(F32)
         far_sum(half, 1)
+    for copy in pc_copies:
+        copy.wait_recv()
+    heads_queries(1)
     heads_send(1)
     for half in range(2):
         third[half].wait_recv()
         gath[B_EARLY, half, :, y, zl] = (part[half] + rf[half, 1].astype(F32)).astype(BF)
     gather_first(B_EARLY)
+    gather_last(B_EARLY)
     gather_end(W_EARLY)
-    gather_last(B_EARLY)
     forward(0, W_EARLY)
     back_queries(0, W_EARLY)
+    exchange(0, 0, query_part)
     heads_end(1)
+    heads_queries(0)
     gather_end(B_EARLY)
 
-    second(0, B_EARLY)
-    back_rest(0, W_EARLY, B_EARLY)
-    exchange(0)
+    for m in range(3):
+        sides(0, B_EARLY, m)
+    second(0)
+    back_sides(0, B_EARLY)
+    back_rest(0, W_EARLY)
+    exchange(0, 1, rest_part)
     heads_send(0)
     heads_end(0)
 
@@ -456,6 +476,7 @@
         pltpu.VMEM((2, 9, T, F), BF),
         pltpu.VMEM((2, 3, 4, 4, 16, 256), F32),
         pltpu.VMEM((2, 3, 4, 4, 16, 256), BF),
+        pltpu.VMEM((4, DH, T), BF),
         pltpu.VMEM((2, 3, 3, 4, 16, 256), BF),
         pltpu.VMEM((2, 3, 4, 16, 256), F32),
         pltpu.VMEM((2, 3, 4, 16, 256), BF),
@@ -465,11 +486,13 @@
         pltpu.VMEM((2, 2, 3, 16, 256), BF),
         pltpu.VMEM((2, T, 3 * DH), BF),
         pltpu.VMEM((2, T, 3 * DH), BF),
+        pltpu.VMEM((2, T, DH), F32),
+        pltpu.VMEM((4, T, DH), F32),
         pltpu.VMEM((2, 3, T, DH), BF),
         pltpu.VMEM((2, 3, T, DH), BF),
         dma((9,)),
     ]
-    for shape in ((2, 7), (2, 4), (4, 2, 3), (4, 2, 3), (2, 3, 3), (2, 3), (2, 2), (6,), (2, 3)):
+    for shape in ((2, 7), (2, 4), (4, 2, 3), (4, 2, 3), (2, 3, 3), (2, 3), (2, 2), (4,), (2, 2), (2, 3)):
         scratch += [dma(shape), dma(shape)]
     return pl.pallas_call(
         kernel,

time: 88.7 us -> 88.9 us (level)
  no operation moved by 1% of the time
where the time goes in v7:
time: 88.9 us; the launch traced here: 88.8 us
  Pallas kernels  86.4 us (97%)
  local copies, waits for them, and re-layouts  1.67 us (2%)
    pallas_call x1, Pallas kernels, local(): pl.pallas_call(kernel, name='meta_gradient', out_shape=jax.ShapeDtypeStru...  86.4 us

profile of v7, /device:TPU:1, one launch (start us, length us, event | category | flops | bytes accessed | tf_op | source)
XLA Modules:
  0.0 88.8 jit_solution(10109645607131798732)
XLA Ops:
  0.7 86.4 %meta_gradient.1 = bf16[2,256,256]{2,1,0:T(8,128)(2,1)} custom-call(bf16[2,256,256]{2,1,0:T(8,128)(2,1)} %xin.1, bf16[2048,256]{1,0:T(8,128)(2,1)} %pq.1, bf16[2048,256]{1,0:T(8,128)(2,1)} %pk.1, bf16[2048,256]{1,0:T(8,128)(2,1)} %pv.1, bf16[2,3,4,512]{3,2,1,0:T(4,128)(2,1)} %bitcast.2, bf16[2,256,256]{2,1,0:T(8,128)(2,1)} %og.1, f32[3,4,512]{2,1,0:T(4,128)} %bitcast.3, ...), custom_call_target="tpu_custom_call" | custom-call | tf_op jit(solution)/shard_map/meta_gradient/pallas_call | solution.py:497
  87.1 1.7 %copy.11 = bf16[2,256,256]{2,1,0:T(8,128)(2,1)} copy(bf16[2,256,256]{2,1,0:T(8,128)(2,1)} %meta_gradient.1) | data formatting | bytes 524288
